TPU v7x, 128 devices: a whole 4x4x4 slice. The times are simulated.
128 devices in a mesh: width: 4 (over z), row: 4 (over y), src: 8 (over x, core).
Axes of the slice: x: 4, y: 4, z: 4, core: 2. Of those that a mesh axis runs over, the one named last changes fastest.
Arguments:
- query_rows: bfloat16 [1024, 8192], P('row', 'width'), may hold values from -150 to 150
- key_rows: bfloat16 [1024, 1024], P('src', 'width'), may hold values from -7 to 7
- value_rows: bfloat16 [1024, 1024], P('src'), may hold values from -6 to 6
- out_proj: bfloat16 [8192, 8192], P(('row', 'src'), 'width'), may hold values from -0.0625 to 0.0625
Outputs:
- share: float32 [1024, 1024], P('row', ('src', 'width'))
All inputs are finite; a program needn't handle non-finite values.
Results may differ from a plain program's by a relative error of at most 0.0014.
Values may be sent and summed in bfloat16 or wider, within the bound.
A program may use at most 192 MiB of HBM per device.

v0:
```python
import math

import jax
import jax.numpy as jnp
from jax import lax
from jax.sharding import PartitionSpec as P

H = 64
KV = 8
HD = 128


def sent_to_all(shard, axis):
    copies = jnp.broadcast_to(shard, (lax.axis_size(axis), *shard.shape))
    return lax.all_to_all(copies, axis, split_axis=0, concat_axis=0, tiled=True)


def gathered_once(shard, axis):
    leaves = jax.tree.leaves(shard)
    sequence = sorted(range(len(leaves)), key=lambda k: -leaves[k].size)
    width = (1, *leaves[sequence[0]].shape)[-1]
    lines = [
        jnp.pad(leaves[k].reshape(-1), (0, -leaves[k].size % width)).reshape(-1, width)
        for k in sequence
    ]
    both, at, found = (sent_to_all(jnp.concatenate(lines), axis), 0, {})
    for k, line in zip(sequence, lines):
        slab = both[:, at : at + len(line)].reshape(len(both), -1)
        found[k] = slab[:, : leaves[k].size].reshape(-1, *leaves[k].shape)
        at += len(line)
    numbers = iter(range(len(leaves)))
    return jax.tree.map(lambda _: found[next(numbers)], shard)


def combined_pairwise(pieces, combine):
    while len(jax.tree.leaves(pieces)[0]) > 1:
        pieces = jax.vmap(combine)(
            *(jax.tree.map(lambda part: part[side::2], pieces) for side in (0, 1))
        )
    return jax.tree.map(lambda part: part[0], pieces)


def merged(shard, axis, combine):
    pieces = gathered_once(shard, axis)
    return combined_pairwise(pieces, combine)


def cut_along(shard, dim, size):
    dims = shard.shape
    parts = shard.reshape(*dims[:dim], size, dims[dim] // size, *dims[dim + 1 :])
    return jnp.moveaxis(parts, dim, 0)


def sum_at_owner(shard, axis, dim):
    size = lax.axis_size(axis)
    parts = lax.all_to_all(cut_along(shard, dim, size), axis, 0, 0, tiled=True)
    return jnp.sum(parts, axis=0)


def of_everyone(shard, axis):
    return sent_to_all(shard, axis).sum(axis=0)


def combine_stats(first, second):
    peak_one, mass_one = first
    peak_two, mass_two = second
    larger = jnp.maximum(peak_one, peak_two)
    return (larger, mass_one * jnp.exp(peak_one - larger) + mass_two * jnp.exp(peak_two - larger))


def body(query_rows, key_rows, value_rows, out_proj):
    here_row = lax.axis_index("row")
    here_src = lax.axis_index("src")
    row_count = query_rows.shape[0]
    col_count = key_rows.shape[0]
    group_size = H // KV
    row_pos = here_row * row_count + jnp.arange(row_count, dtype=jnp.int32)
    col_pos = here_src * col_count + jnp.arange(col_count, dtype=jnp.int32)
    local_heads = query_rows.shape[1] // HD
    local_kv = key_rows.shape[1] // HD
    queries = query_rows.reshape(row_count, local_kv, group_size, HD)
    key_heads = key_rows.reshape(col_count, local_kv, HD)
    scores = jnp.einsum("ikgd,jkd->kgij", queries, key_heads, preferred_element_type=jnp.float32)
    scores = scores.reshape(local_heads, row_count, col_count) / jnp.sqrt(jnp.float32(HD))
    causal = row_pos[:, None] >= col_pos[None, :]
    masked = jnp.where(causal, scores, jnp.float32(-1e30))
    row_peak = jnp.max(masked, axis=-1)
    row_mass = jnp.sum(jnp.where(causal, jnp.exp(masked - row_peak[..., None]), 0.0), axis=-1)
    row_peak, row_mass = merged((row_peak, row_mass), "src", combine_stats)
    weights = jnp.where(
        causal, jnp.exp(masked - row_peak[..., None]) / row_mass[..., None], 0.0
    ).astype(jnp.bfloat16)
    weights = lax.all_gather(weights, "width", axis=0, tiled=True)
    value_heads = value_rows.reshape(col_count, KV, HD)
    out_cols = out_proj.shape[1]
    proj_heads = out_proj.reshape(-1, HD, out_cols)
    portion = lax.all_gather(proj_heads, ("row", "src"), axis=0, tiled=True)
    head_count = portion.shape[0]
    head_ids = jnp.arange(head_count, dtype=jnp.int32)
    selector = (head_ids[:, None] // group_size == jnp.arange(KV, dtype=jnp.int32)[None, :]).astype(
        jnp.bfloat16
    )
    chosen = jnp.einsum(
        "hk,jkd->jhd", selector, value_heads, preferred_element_type=jnp.float32
    ).astype(jnp.bfloat16)
    images = jnp.einsum("jhd,hde->jhe", chosen, portion, preferred_element_type=jnp.float32).astype(
        jnp.bfloat16
    )
    row_block = math.gcd(row_count, 64)
    col_block = math.gcd(col_count, 32)
    col_steps = col_count // col_block
    turns = row_count // row_block * col_steps

    def tile(turn_index, running):
        row_start = turn_index // col_steps * row_block
        col_start = turn_index % col_steps * col_block
        row_slice = lax.dynamic_slice_in_dim(row_pos, row_start, row_block)
        col_slice = lax.dynamic_slice_in_dim(col_pos, col_start, col_block)

        def compute(unused):
            attend = lax.dynamic_slice(
                weights, (0, row_start, col_start), (H, row_block, col_block)
            )
            source_images = lax.dynamic_slice_in_dim(images, col_start, col_block, 0)
            contrib = jnp.einsum(
                "hij,jhe->ije", attend, source_images, preferred_element_type=jnp.float32
            )
            return jnp.sum(jnp.abs(contrib), axis=-1)

        def skipped(unused):
            return jnp.zeros((row_block, col_block), jnp.float32)

        result = lax.cond(jnp.max(row_slice) >= jnp.min(col_slice), compute, skipped, 0)
        return lax.dynamic_update_slice(running, result, (row_start, col_start))

    partial_value = lax.fori_loop(0, turns, tile, jnp.zeros((row_count, col_count), jnp.float32))
    summed = sum_at_owner(partial_value, "width", 1)
    totals = of_everyone(jnp.sum(summed, axis=1), ("width", "src"))
    position = (here_row * row_count + jnp.arange(row_count, dtype=jnp.int32) + 1).astype(
        jnp.float32
    )
    return position[:, None] * summed / totals[:, None]


def solution(mesh):
    placed = (P("row", "width"), P("src", "width"), P("src", None), P(("row", "src"), "width"))
    return jax.shard_map(
        body, mesh=mesh, in_specs=placed, out_specs=P("row", ("src", "width")), check_vma=False
    )
```

profile of v0, /device:TPU:25, one launch (start us, length us, event | category | flops | bytes accessed | tf_op | source)
XLA Modules:
  0.0 431.4 jit_solution(18067964968503341397)
XLA Ops:
  27.2 47.7 %all-gather.5.cloned.1.call-done = bf16[64,256,128]{2,1,0:T(8,128)(2,1)} async-done(((bf16[16,256,128]{2,1,0:T(8,128)(2,1)}), bf16[64,256,128]{2,1,0:T(8,128)(2,1)}) %all-gather.5.cloned.1.call-update) | async-done | bytes 4194320 | tf_op jit(solution)/shard_map/all_gather | solution.py:93
  75.0 15.6 %copy.29 = bf16[64,256,128]{0,1,2:T(8,128)(2,1)} copy(bf16[64,256,128]{2,1,0:T(8,128)(2,1)} %all-gather.5.cloned.1.call-done) | data formatting | bytes 8388608 | tf_op jit(solution)/shard_map/while | solution.py:136
  90.6 100.2 %all-gather.3.cloned.1.call-done = bf16[64,128,2048]{2,1,0:T(8,128)(2,1)} async-done(((bf16[2,128,2048]{2,1,0:T(8,128)(2,1)}), bf16[64,128,2048]{2,1,0:T(8,128)(2,1)}) %all-gather.3.cloned.1.call-update) | async-done | bytes 33554448 | tf_op jit(solution)/shard_map/all_gather | solution.py:97
  190.8 24.2 %convert_bitcast_fusion = bf16[128,64,2048]{2,0,1:T(8,128)(2,1)} fusion(bf16[64,128,2048]{2,1,0:T(8,128)(2,1)} %all-gather.3.cloned.1.call-done, bf16[128,64,128]{2,1,0:T(8,128)(2,1)S(1)} %convert_bitcast_fusion.1), kind=kOutput, calls=%fused_computation.7 | convolution fusion | flops 4311744512 | bytes 69206016 | tf_op jit(solution)/shard_map/jhd,hde->jhe/dot_general | solution.py:106
  215.0 30.0 %copy.28 = bf16[128,64,2048]{2,1,0:T(8,128)(2,1)} copy(bf16[128,64,2048]{2,0,1:T(8,128)(2,1)} %convert_bitcast_fusion) | data formatting | bytes 67108864 | tf_op jit(solution)/shard_map/while | solution.py:136
  245.0 156.7 %while.15 = (s32[]{:T(128)}, f32[256,128]{0,1:T(8,128)S(1)}, s32[256]{0:T(256)S(1)}, s32[128]{0:T(128)S(1)}, bf16[128,64,2048]{2,1,0:T(8,128)(2,1)}, /*index=5*/...) while((s32[]{:T(128)}, f32[256,128]{0,1:T(8,128)S(1)}, ...), condition=%wide.region_8.9_spmd, body=%wide.region_2.8_spmd.sunk | while | flops 545257600 | bytes 8939898 | solution.py:136
  247.9 6.0 %conditional.2 = (f32[64,32]{0,1:T(8,128)S(1)}) conditional(s32[]{:T(128)} %convert_element_type.44, () %tuple.54, (s32[]{:T(128)}, bf16[128,64,2048]{2,1,0:T(8,128)(2,1)}, s32[]{:T(128)}, bf16[64,256,128]{0,1,2:T(8,128)(2,1)}) %tuple.55), branch_computations={%region_5.5_spmd, %region_6.7_spmd} | conditional | flops 545257472 | bytes 8922700 | solution.py:133
  247.9 6.0 %abs_reduce_fusion = f32[32,64]{1,0:T(8,128)S(1)} fusion(bf16[128,64,2048]{2,1,0:T(8,128)(2,1)} %get-tuple-element.172, s32[]{:T(128)S(6)} %select_n.76, bf16[64,256,128]{0,1,2:T(8,128)(2,1)} %get-tuple-element.174, s32[]{:T(128)S(6)} %select_n.77), kind=kOutput, calls=%fused_computation | convolution fusion | flops 545257472 | bytes 8922624 | tf_op jit(solution)/shard_map/while/body/eval_jaxpr/cond/branch_1_fun/hij,jhe->ije/dot_general | solution.py:125
  257.7 6.0 %conditional.2 = (f32[64,32]{0,1:T(8,128)S(1)}) conditional(s32[]{:T(128)} %convert_element_type.44, () %tuple.54, (s32[]{:T(128)}, bf16[128,64,2048]{2,1,0:T(8,128)(2,1)}, s32[]{:T(128)}, bf16[64,256,128]{0,1,2:T(8,128)(2,1)}) %tuple.55), branch_computations={%region_5.5_spmd, %region_6.7_spmd} | conditional | flops 545257472 | bytes 8922700 | solution.py:133
  257.7 6.0 %abs_reduce_fusion = f32[32,64]{1,0:T(8,128)S(1)} fusion(bf16[128,64,2048]{2,1,0:T(8,128)(2,1)} %get-tuple-element.172, s32[]{:T(128)S(6)} %select_n.76, bf16[64,256,128]{0,1,2:T(8,128)(2,1)} %get-tuple-element.174, s32[]{:T(128)S(6)} %select_n.77), kind=kOutput, calls=%fused_computation | convolution fusion | flops 545257472 | bytes 8922624 | tf_op jit(solution)/shard_map/while/body/eval_jaxpr/cond/branch_1_fun/hij,jhe->ije/dot_general | solution.py:125
  267.5 6.0 %conditional.2 = (f32[64,32]{0,1:T(8,128)S(1)}) conditional(s32[]{:T(128)} %convert_element_type.44, () %tuple.54, (s32[]{:T(128)}, bf16[128,64,2048]{2,1,0:T(8,128)(2,1)}, s32[]{:T(128)}, bf16[64,256,128]{0,1,2:T(8,128)(2,1)}) %tuple.55), branch_computations={%region_5.5_spmd, %region_6.7_spmd} | conditional | flops 545257472 | bytes 8922700 | solution.py:133
  267.5 6.0 %abs_reduce_fusion = f32[32,64]{1,0:T(8,128)S(1)} fusion(bf16[128,64,2048]{2,1,0:T(8,128)(2,1)} %get-tuple-element.172, s32[]{:T(128)S(6)} %select_n.76, bf16[64,256,128]{0,1,2:T(8,128)(2,1)} %get-tuple-element.174, s32[]{:T(128)S(6)} %select_n.77), kind=kOutput, calls=%fused_computation | convolution fusion | flops 545257472 | bytes 8922624 | tf_op jit(solution)/shard_map/while/body/eval_jaxpr/cond/branch_1_fun/hij,jhe->ije/dot_general | solution.py:125
  277.3 6.0 %conditional.2 = (f32[64,32]{0,1:T(8,128)S(1)}) conditional(s32[]{:T(128)} %convert_element_type.44, () %tuple.54, (s32[]{:T(128)}, bf16[128,64,2048]{2,1,0:T(8,128)(2,1)}, s32[]{:T(128)}, bf16[64,256,128]{0,1,2:T(8,128)(2,1)}) %tuple.55), branch_computations={%region_5.5_spmd, %region_6.7_spmd} | conditional | flops 545257472 | bytes 8922700 | solution.py:133
  277.3 6.0 %abs_reduce_fusion = f32[32,64]{1,0:T(8,128)S(1)} fusion(bf16[128,64,2048]{2,1,0:T(8,128)(2,1)} %get-tuple-element.172, s32[]{:T(128)S(6)} %select_n.76, bf16[64,256,128]{0,1,2:T(8,128)(2,1)} %get-tuple-element.174, s32[]{:T(128)S(6)} %select_n.77), kind=kOutput, calls=%fused_computation | convolution fusion | flops 545257472 | bytes 8922624 | tf_op jit(solution)/shard_map/while/body/eval_jaxpr/cond/branch_1_fun/hij,jhe->ije/dot_general | solution.py:125
  286.9 6.0 %conditional.2 = (f32[64,32]{0,1:T(8,128)S(1)}) conditional(s32[]{:T(128)} %convert_element_type.44, () %tuple.54, (s32[]{:T(128)}, bf16[128,64,2048]{2,1,0:T(8,128)(2,1)}, s32[]{:T(128)}, bf16[64,256,128]{0,1,2:T(8,128)(2,1)}) %tuple.55), branch_computations={%region_5.5_spmd, %region_6.7_spmd} | conditional | flops 545257472 | bytes 8922700 | solution.py:133
  286.9 6.0 %abs_reduce_fusion = f32[32,64]{1,0:T(8,128)S(1)} fusion(bf16[128,64,2048]{2,1,0:T(8,128)(2,1)} %get-tuple-element.172, s32[]{:T(128)S(6)} %select_n.76, bf16[64,256,128]{0,1,2:T(8,128)(2,1)} %get-tuple-element.174, s32[]{:T(128)S(6)} %select_n.77), kind=kOutput, calls=%fused_computation | convolution fusion | flops 545257472 | bytes 8922624 | tf_op jit(solution)/shard_map/while/body/eval_jaxpr/cond/branch_1_fun/hij,jhe->ije/dot_general | solution.py:125
  297.0 6.0 %conditional.2 = (f32[64,32]{0,1:T(8,128)S(1)}) conditional(s32[]{:T(128)} %convert_element_type.44, () %tuple.54, (s32[]{:T(128)}, bf16[128,64,2048]{2,1,0:T(8,128)(2,1)}, s32[]{:T(128)}, bf16[64,256,128]{0,1,2:T(8,128)(2,1)}) %tuple.55), branch_computations={%region_5.5_spmd, %region_6.7_spmd} | conditional | flops 545257472 | bytes 8922700 | solution.py:133
  307.0 6.0 %conditional.2 = (f32[64,32]{0,1:T(8,128)S(1)}) conditional(s32[]{:T(128)} %convert_element_type.44, () %tuple.54, (s32[]{:T(128)}, bf16[128,64,2048]{2,1,0:T(8,128)(2,1)}, s32[]{:T(128)}, bf16[64,256,128]{0,1,2:T(8,128)(2,1)}) %tuple.55), branch_computations={%region_5.5_spmd, %region_6.7_spmd} | conditional | flops 545257472 | bytes 8922700 | solution.py:133
  317.1 6.0 %conditional.2 = (f32[64,32]{0,1:T(8,128)S(1)}) conditional(s32[]{:T(128)} %convert_element_type.44, () %tuple.54, (s32[]{:T(128)}, bf16[128,64,2048]{2,1,0:T(8,128)(2,1)}, s32[]{:T(128)}, bf16[64,256,128]{0,1,2:T(8,128)(2,1)}) %tuple.55), branch_computations={%region_5.5_spmd, %region_6.7_spmd} | conditional | flops 545257472 | bytes 8922700 | solution.py:133
  327.0 6.0 %conditional.2 = (f32[64,32]{0,1:T(8,128)S(1)}) conditional(s32[]{:T(128)} %convert_element_type.44, () %tuple.54, (s32[]{:T(128)}, bf16[128,64,2048]{2,1,0:T(8,128)(2,1)}, s32[]{:T(128)}, bf16[64,256,128]{0,1,2:T(8,128)(2,1)}) %tuple.55), branch_computations={%region_5.5_spmd, %region_6.7_spmd} | conditional | flops 545257472 | bytes 8922700 | solution.py:133
  327.0 6.0 %abs_reduce_fusion = f32[32,64]{1,0:T(8,128)S(1)} fusion(bf16[128,64,2048]{2,1,0:T(8,128)(2,1)} %get-tuple-element.172, s32[]{:T(128)S(6)} %select_n.76, bf16[64,256,128]{0,1,2:T(8,128)(2,1)} %get-tuple-element.174, s32[]{:T(128)S(6)} %select_n.77), kind=kOutput, calls=%fused_computation | convolution fusion | flops 545257472 | bytes 8922624 | tf_op jit(solution)/shard_map/while/body/eval_jaxpr/cond/branch_1_fun/hij,jhe->ije/dot_general | solution.py:125
  336.6 6.0 %conditional.2 = (f32[64,32]{0,1:T(8,128)S(1)}) conditional(s32[]{:T(128)} %convert_element_type.44, () %tuple.54, (s32[]{:T(128)}, bf16[128,64,2048]{2,1,0:T(8,128)(2,1)}, s32[]{:T(128)}, bf16[64,256,128]{0,1,2:T(8,128)(2,1)}) %tuple.55), branch_computations={%region_5.5_spmd, %region_6.7_spmd} | conditional | flops 545257472 | bytes 8922700 | solution.py:133
  346.2 6.0 %conditional.2 = (f32[64,32]{0,1:T(8,128)S(1)}) conditional(s32[]{:T(128)} %convert_element_type.44, () %tuple.54, (s32[]{:T(128)}, bf16[128,64,2048]{2,1,0:T(8,128)(2,1)}, s32[]{:T(128)}, bf16[64,256,128]{0,1,2:T(8,128)(2,1)}) %tuple.55), branch_computations={%region_5.5_spmd, %region_6.7_spmd} | conditional | flops 545257472 | bytes 8922700 | solution.py:133
  346.2 6.0 %abs_reduce_fusion = f32[32,64]{1,0:T(8,128)S(1)} fusion(bf16[128,64,2048]{2,1,0:T(8,128)(2,1)} %get-tuple-element.172, s32[]{:T(128)S(6)} %select_n.76, bf16[64,256,128]{0,1,2:T(8,128)(2,1)} %get-tuple-element.174, s32[]{:T(128)S(6)} %select_n.77), kind=kOutput, calls=%fused_computation | convolution fusion | flops 545257472 | bytes 8922624 | tf_op jit(solution)/shard_map/while/body/eval_jaxpr/cond/branch_1_fun/hij,jhe->ije/dot_general | solution.py:125
  355.8 6.0 %conditional.2 = (f32[64,32]{0,1:T(8,128)S(1)}) conditional(s32[]{:T(128)} %convert_element_type.44, () %tuple.54, (s32[]{:T(128)}, bf16[128,64,2048]{2,1,0:T(8,128)(2,1)}, s32[]{:T(128)}, bf16[64,256,128]{0,1,2:T(8,128)(2,1)}) %tuple.55), branch_computations={%region_5.5_spmd, %region_6.7_spmd} | conditional | flops 545257472 | bytes 8922700 | solution.py:133
  355.8 6.0 %abs_reduce_fusion = f32[32,64]{1,0:T(8,128)S(1)} fusion(bf16[128,64,2048]{2,1,0:T(8,128)(2,1)} %get-tuple-element.172, s32[]{:T(128)S(6)} %select_n.76, bf16[64,256,128]{0,1,2:T(8,128)(2,1)} %get-tuple-element.174, s32[]{:T(128)S(6)} %select_n.77), kind=kOutput, calls=%fused_computation | convolution fusion | flops 545257472 | bytes 8922624 | tf_op jit(solution)/shard_map/while/body/eval_jaxpr/cond/branch_1_fun/hij,jhe->ije/dot_general | solution.py:125
  365.2 6.0 %conditional.2 = (f32[64,32]{0,1:T(8,128)S(1)}) conditional(s32[]{:T(128)} %convert_element_type.44, () %tuple.54, (s32[]{:T(128)}, bf16[128,64,2048]{2,1,0:T(8,128)(2,1)}, s32[]{:T(128)}, bf16[64,256,128]{0,1,2:T(8,128)(2,1)}) %tuple.55), branch_computations={%region_5.5_spmd, %region_6.7_spmd} | conditional | flops 545257472 | bytes 8922700 | solution.py:133
  375.1 6.0 %conditional.2 = (f32[64,32]{0,1:T(8,128)S(1)}) conditional(s32[]{:T(128)} %convert_element_type.44, () %tuple.54, (s32[]{:T(128)}, bf16[128,64,2048]{2,1,0:T(8,128)(2,1)}, s32[]{:T(128)}, bf16[64,256,128]{0,1,2:T(8,128)(2,1)}) %tuple.55), branch_computations={%region_5.5_spmd, %region_6.7_spmd} | conditional | flops 545257472 | bytes 8922700 | solution.py:133
  384.9 6.0 %conditional.2 = (f32[64,32]{0,1:T(8,128)S(1)}) conditional(s32[]{:T(128)} %convert_element_type.44, () %tuple.54, (s32[]{:T(128)}, bf16[128,64,2048]{2,1,0:T(8,128)(2,1)}, s32[]{:T(128)}, bf16[64,256,128]{0,1,2:T(8,128)(2,1)}) %tuple.55), branch_computations={%region_5.5_spmd, %region_6.7_spmd} | conditional | flops 545257472 | bytes 8922700 | solution.py:133
  394.8 6.0 %conditional.2 = (f32[64,32]{0,1:T(8,128)S(1)}) conditional(s32[]{:T(128)} %convert_element_type.44, () %tuple.54, (s32[]{:T(128)}, bf16[128,64,2048]{2,1,0:T(8,128)(2,1)}, s32[]{:T(128)}, bf16[64,256,128]{0,1,2:T(8,128)(2,1)}) %tuple.55), branch_computations={%region_5.5_spmd, %region_6.7_spmd} | conditional | flops 545257472 | bytes 8922700 | solution.py:133
  401.7 8.7 %all_to_all.16 = f32[4,256,32]{1,2,0:T(8,128)S(1)} all-to-all(f32[4,256,32]{1,2,0:T(8,128)S(1)} %bitcast.40), channel_id=1, replica_groups=mesh['width'=4,'row'=4,'src'=8] {'width'}, dimensions={0} | all-to-all | bytes 262144 | tf_op jit(solution)/shard_map/all_to_all | solution.py:56
  416.6 7.2 %all-to-all-done.2 = f32[32,1,256]{2,1,0:T(1,128)S(1)} async-done(((f32[32,1,256]{2,1,0:T(1,128)}), f32[32,1,256]{2,1,0:T(1,128)S(1)}, u32[]{:S(2)}, u32[]{:S(2)}) %all-to-all-start.2) | async-done | bytes 32800 | tf_op jit(solution)/shard_map/all_to_all | solution.py:15
  (92 shorter events, 113.9 us)
Async XLA Ops:
  6.5 1.5 copy-start.1
  10.0 11.5 %all-to-all-start = ((f32[8,32,256]{2,1,0:T(8,128)}), f32[8,32,256]{2,1,0:T(8,128)S(1)}, u32[]{:S(2)}, u32[]{:S(2)}) async-start(f32[8,32,256]{2,1,0:T(8,128)} %broadcast_in_dim.44), calls=%async_computation | async-start | bytes 524288 | tf_op jit(solution)/shard_map/all_to_all | solution.py:15
  14.9 60.0 %all-gather.5.cloned.1.call-start = ((), (), s32[]{:S(2)}) async-start(), calls=%async_computation.4 | async-start | bytes 5242880 | tf_op jit(solution)/shard_map/all_gather | solution.py:93
  21.6 4.9 %copy-start = (bf16[128,1024]{1,0:T(8,128)(2,1)S(1)}, bf16[128,1024]{1,0:T(8,128)(2,1)}, u32[]{:S(2)}) copy-start(bf16[128,1024]{1,0:T(8,128)(2,1)} %param.10) | copy-start | bytes 786436
  25.7 165.1 %all-gather.3.cloned.1.call-start = ((), (), s32[]{:S(2)}) async-start(), calls=%async_computation.3 | async-start | bytes 34603008 | tf_op jit(solution)/shard_map/all_gather | solution.py:97
  411.1 12.8 %all-to-all-start.2 = ((f32[32,1,256]{2,1,0:T(1,128)}), f32[32,1,256]{2,1,0:T(1,128)S(1)}, u32[]{:S(2)}, u32[]{:S(2)}) async-start(f32[32,1,256]{2,1,0:T(1,128)} %broadcast_in_dim.46), calls=%async_computation.2 | async-start | bytes 65536 | tf_op jit(solution)/shard_map/all_to_all | solution.py:15
Sparse Core Ops, SparseCore 0:
  25.8 49.1 all-gather.4
  77.2 113.4 all-gather.2
where the time goes:
time: 432 us; the launch traced here: 431 us
  waiting for transfers between devices  160 us (37%)
  matrix products  122 us (28%)
  local copies, waits for them, and re-layouts  64.2 us (15%)
  other arithmetic  30.2 us (7%)
  loops' own time  22.2 us (5%)
  between operations  13.6 us (3%)
  starting transfers between devices  10.8 us (2%)
  blocking collectives  8.75 us (2%)
    all_gather x1, waiting for transfers between devices, body(): portion = lax.all_gather(proj_heads, ('row', 'src'), axis=0, tiled=True)  100 us
    dot_general x16, matrix products, compute(): jnp.einsum('hij,jhe->ije', attend, source_images, preferred_element_type=...  96.1 us
    all_gather x1, waiting for transfers between devices, body(): weights = lax.all_gather(weights, 'width', axis=0, tiled=True)  47.7 us
    while x2, local copies, waits for them, and re-layouts, body(): lax.fori_loop(0, turns, tile, jnp.zeros((row_count, col_count), jnp.float...  45.6 us
    dot_general x1, matrix products, body(): jnp.einsum('jhd,hde->jhe', chosen, portion, preferred_element_type=jnp.fl...  24.2 us
    another operation x1, loops' own time, body(): lax.fori_loop(0, turns, tile, jnp.zeros((row_count, col_count), jnp.float...  21.8 us
    dynamic_update_slice x16, local copies, waits for them, and re-layouts, tile(): return lax.dynamic_update_slice(running, result, (row_start, col_start))  13.7 us
    reduce_max x16, other arithmetic, tile(): jnp.max(row_slice) >= jnp.min(col_slice)  12.5 us
  transfers between devices with their start and end apart: 4, of which 4 were waited for; matrix products, arithmetic and copies ran while one was open for 4% of the time, Pallas kernels for 0%

commit v1 on v0

v1 whole, which is shorter than its diff:
```python
import math
import jax, jax.numpy as jnp
from jax import lax
from jax.experimental import pallas as pl
from jax.experimental.pallas import tpu as pltpu
from jax.sharding import PartitionSpec as PS_
C2 = math.log2(math.e) / math.sqrt(128.0)
F32, BF = jnp.float32, jnp.bfloat16
NEG = -1e30
PS, IS = 17, 65

def pair_of(y):
    return jnp.where(y == 0, 0, jnp.where(y == 3, 1, y + 1))

def kernel_b(q, k, v, o, out, P, W, MS, LS, FS, IM):
    p = pair_of(lax.axis_index("row"))
    big = 7 - p
    jl = lax.broadcasted_iota(jnp.int32, (128, 256), 0)
    il = lax.broadcasted_iota(jnp.int32, (128, 256), 1) % 128

    def scores(zc, slot, ib, base):
        MS[...] = jnp.full(MS.shape, NEG, F32)
        LS[...] = jnp.zeros(LS.shape, F32)

        def block(jb, diag):
            for hp in range(8):
                kk = k[zc, pl.ds(pl.multiple_of(jb * 128, 128), 128), (hp // 4) * 128:(hp // 4 + 1) * 128]
                qq = jnp.concatenate([q[zc, slot * 128:(slot + 1) * 128, (2 * hp + a) * 128:(2 * hp + a + 1) * 128] for a in (0, 1)], axis=0)
                s = lax.dot_general(kk, qq, (((1,), (1,)), ((), ())), preferred_element_type=F32)
                if diag:
                    s = jnp.where(jl <= il, s, NEG)
                m = jnp.max(s, axis=0, keepdims=True)
                e = jnp.exp2((s - m) * C2)
                l = jnp.sum(e, axis=0, keepdims=True)
                for a in (0, 1):
                    lanes = slice(a * 128, (a + 1) * 128)
                    P[jb, pl.ds(2 * hp + a, 128, stride=PS), :] = e[:, lanes]
                    MS[jb, 2 * hp + a:2 * hp + a + 1, :] = m[:, lanes]
                    LS[jb, 2 * hp + a:2 * hp + a + 1, :] = l[:, lanes]

        def plain(jb, c):
            block(jb, False)
            return c
        lax.fori_loop(0, ib, plain, 0)
        block(ib, True)
        ms = MS[...]
        f = jnp.exp2((ms - jnp.max(ms, axis=0, keepdims=True)) * C2)
        z = jnp.sum(f * LS[...], axis=0, keepdims=True)
        FS[...] = f / z

        def conv(jb, c):
            f = FS[jb]
            for j in range(128):
                x = P[jb, j * PS:j * PS + 16, :] * f
                W[base + jb, j, pl.ds(pl.multiple_of(zc * 16, 16), 16), :] = x.astype(BF)
            return c
        lax.fori_loop(0, ib + 1, conv, 0)

    def zstep(zc, c):
        scores(zc, 0, p, big + 1)
        scores(zc, 1, big, 0)
        return c
    lax.fori_loop(0, 4, zstep, 0)

    out[...] = jnp.zeros(out.shape, F32)

    def jstep(jb, c):
        def img(g, c):
            vvs = [v[pl.ds(pl.multiple_of(jb * 128, 128), 128), pl.ds(pl.multiple_of(g * 256 + b * 128, 128), 128)] for b in (0, 1)]
            for hh in range(16):
                h = g * 16 + hh
                oo = o[pl.ds(pl.multiple_of(h * 128, 128), 128), :]
                x = jnp.dot(vvs[hh // 8], oo, preferred_element_type=F32)
                for a in (0, 1):
                    IM[a, pl.ds(h, 128, stride=IS), :] = x[:, a * 128:(a + 1) * 128]
            return c
        lax.fori_loop(0, 4, img, 0)

        def contrib(t, slot):
            zero = jnp.zeros((64, 128), BF)
            PU = 32

            def pairs(n, c):
                rows = []
                for u in range(PU):
                    j = n * (2 * PU) + 2 * u
                    r0 = pl.multiple_of(n * (2 * PU * IS), 8)
                    lhs = jnp.concatenate([jnp.concatenate([IM[a, pl.ds(r0 + (2 * u + b) * IS, 64), :].astype(BF) for b in (0, 1)], axis=0) for a in (0, 1)], axis=1)
                    rhs = jnp.concatenate([
                        jnp.concatenate([W[t, j], zero], axis=1),
                        jnp.concatenate([zero, W[t, j + 1]], axis=1)], axis=0)
                    cc = lax.dot_general(lhs, rhs, (((0,), (0,)), ((), ())), preferred_element_type=F32)
                    r = jnp.sum(jnp.abs(cc), axis=0, keepdims=True)
                    rows += [r[:, :128], r[:, 128:]]
                for b in range(PU // 4):
                    out[slot, pl.ds(pl.multiple_of(jb * 128 + n * (2 * PU) + 8 * b, 8), 8), :] = jnp.concatenate(rows[8 * b:8 * b + 8], axis=0)
                return c
            lax.fori_loop(0, 128 // (2 * PU), pairs, 0)
        contrib(jb, 1)

        @pl.when(jb <= p)
        def _():
            contrib(big + 1 + jb, 0)
        return c
    lax.fori_loop(0, big + 1, jstep, 0)

SCR = [pltpu.VMEM((8, 128 * PS, 128), F32), pltpu.VMEM((9, 128, 64, 128), BF),
       pltpu.VMEM((8, 16, 128), F32), pltpu.VMEM((8, 16, 128), F32), pltpu.VMEM((8, 16, 128), F32),
       pltpu.VMEM((2, 128 * IS, 128), F32)]


def contributions(q, k, v, o):
    vm = pl.BlockSpec(memory_space=pltpu.VMEM)
    return pl.pallas_call(kernel_b, out_shape=jax.ShapeDtypeStruct((2, 1024, 128), F32),
        in_specs=[vm] * 4, out_specs=vm, scratch_shapes=SCR,
        compiler_params=pltpu.CompilerParams(vmem_limit_bytes=62 * 2**20))(q, k, v, o)


PARTNER = [(0, 3), (3, 0), (1, 2), (2, 1)]


def body(query_rows, key_rows, value_rows, out_proj):
    row = lax.axis_index("row")
    low = row < 2
    kept, other = query_rows[:128], lax.ppermute(query_rows[128:], "row", PARTNER)
    small, big = jnp.where(low, kept, other), jnp.where(low, other, kept)
    q = lax.all_gather(jnp.concatenate([small, big], axis=0), "width")
    k = lax.all_gather(lax.all_gather(key_rows, "src", tiled=True), "width")
    v = lax.all_gather(value_rows, "src", tiled=True)
    o = lax.all_to_all(out_proj, "src", 1, 0, tiled=True)
    o = lax.all_gather(o, "row", tiled=True)
    part = contributions(q, k, v, o)
    norms = lax.psum_scatter(part, ("src", "width"), scatter_dimension=1, tiled=True)
    totals = lax.psum(jnp.sum(norms, axis=1), ("src", "width"))
    p = pair_of(row)
    pos = jnp.stack([p, 7 - p])[:, None] * 128 + jnp.arange(1, 129, dtype=jnp.int32)[None, :]
    share = norms * (pos.astype(F32) / totals)[:, None, :]
    share = share.transpose(0, 2, 1)
    kept, other = jnp.where(low, share[0], share[1]), jnp.where(low, share[1], share[0])
    return jnp.concatenate([kept, lax.ppermute(other, "row", PARTNER)], axis=0)


def solution(mesh):
    placed = (PS_("row", "width"), PS_("src", "width"), PS_("src", None), PS_(("row", "src"), "width"))
    return jax.shard_map(
        body, mesh=mesh, in_specs=placed, out_specs=PS_("row", ("src", "width")), check_vma=False
    )
```

time: 432 us -> 398 us (0.921); the launches traced: 431 us -> 392 us
  matrix products: 122 us -> 0 us
  blocking collectives: 8.75 us -> 96.1 us
  local copies, waits for them, and re-layouts: 64.2 us -> 1.52 us
  Pallas kernels: 0 us -> 60.2 us
  waiting for transfers between devices: 160 us -> 217 us
  other arithmetic: 30.2 us -> 3.57 us
  loops' own time: 22.2 us -> 0 us
  starting transfers between devices: 10.8 us -> 0.56 us
    dot_general x19 -> x0, matrix products: 122 us -> none  [the longest x16 96.1 us: compute(): jnp.einsum('hij,jhe->ije', attend, source_images, preferred_element_type=...]
    reduce_scatter x0 -> x1, waiting for transfers between devices: none -> 78.5 us  [body(): lax.psum_scatter(part, ('src', 'width'), scatter_dimension=1, tiled=True)]
    psum x0 -> x1, blocking collectives: none -> 61.2 us  [body(): totals = lax.psum(jnp.sum(norms, axis=1), ('src', 'width'))]
    pallas_call x0 -> x1, Pallas kernels: none -> 60.2 us  [contributions(): pl.pallas_call(kernel_b, out_shape=jax.ShapeDtypeStruct((2, 1024, 128), F...]
    while x2 -> x0, local copies, waits for them, and re-layouts: 45.6 us -> none  [body(): lax.fori_loop(0, turns, tile, jnp.zeros((row_count, col_count), jnp.float...]
    all_gather x2 -> x4, waiting for transfers between devices: 148 us -> 120 us  [the longest x1 50.1 us: body(): q = lax.all_gather(jnp.concatenate([small, big], axis=0), 'width')]
    another operation x17 -> x0, loops' own time: 22.2 us -> none  [the longest x1 21.8 us: body(): lax.fori_loop(0, turns, tile, jnp.zeros((row_count, col_count), jnp.float...]
    ppermute x0 -> x2, waiting for transfers between devices: none -> 18.2 us  [the longest x1 14.7 us: body(): lax.ppermute(query_rows[128:], 'row', PARTNER)]
  transfers between devices with their start and end apart: 4 -> 7, of which waited for: 4 -> 6; matrix products, arithmetic and copies ran while one was open for 4% -> 1% of each run, Pallas kernels for 0% -> 0%
where the time goes in v1:
time: 398 us; the launch traced here: 392 us
  waiting for transfers between devices  217 us (55%)
  blocking collectives  96.1 us (24%)
  Pallas kernels  60.2 us (15%)
  between operations  13.2 us (3%)
    reduce_scatter x1, waiting for transfers between devices, body(): lax.psum_scatter(part, ('src', 'width'), scatter_dimension=1, tiled=True)  78.5 us
    psum x1, blocking collectives, body(): totals = lax.psum(jnp.sum(norms, axis=1), ('src', 'width'))  61.2 us
    pallas_call x1, Pallas kernels, contributions(): pl.pallas_call(kernel_b, out_shape=jax.ShapeDtypeStruct((2, 1024, 128), F...  60.2 us
    all_gather x1, waiting for transfers between devices, body(): q = lax.all_gather(jnp.concatenate([small, big], axis=0), 'width')  50.1 us
    all_gather x1, waiting for transfers between devices, body(): o = lax.all_gather(o, 'row', tiled=True)  48.1 us
    all_gather x1, waiting for transfers between devices, body(): v = lax.all_gather(value_rows, 'src', tiled=True)  21.4 us
    all_to_all x1, blocking collectives, body(): o = lax.all_to_all(out_proj, 'src', 1, 0, tiled=True)  19.5 us
    all_gather x1, blocking collectives, body(): k = lax.all_gather(lax.all_gather(key_rows, 'src', tiled=True), 'width')  15.4 us
  transfers between devices with their start and end apart: 7, of which 6 were waited for; matrix products, arithmetic and copies ran while one was open for 1% of the time, Pallas kernels for 0%

profile of v1, /device:TPU:25, one launch (start us, length us, event | category | flops | bytes accessed | tf_op | source)
XLA Modules:
  0.0 392.2 jit_solution(10789085966518004482)
XLA Ops:
  6.5 15.4 %all_gather.23 = bf16[1024,256]{1,0:T(8,128)(2,1)} all-gather(bf16[128,256]{1,0:T(8,128)(2,1)} %param.5), channel_id=1, replica_groups=mesh['width'=4,'row'=4,'src'=8] {'src'}, dimensions={0}, use_global_device_ids=true | all-gather | bytes 589824 | tf_op jit(solution)/shard_map/all_gather | solution.py:128
  21.9 0.0 all-gather.13.cloned.1.call-update
  21.9 0.0 all-gather.7.cloned.1.call-start
  22.0 0.7 all-gather.7.cloned.1.call-update
  22.7 0.0 all-gather.11.cloned.1.call-start
  22.7 1.1 slice.15
  23.8 0.1 collective-permute-start
  23.9 14.7 %collective-permute-done = bf16[128,2048]{1,0:T(8,128)(2,1)S(1)} collective-permute-done((bf16[128,2048]{1,0:T(8,128)(2,1)S(1)}, bf16[128,2048]{1,0:T(8,128)(2,1)S(1)}, u32[]{:S(2)}, u32[]{:S(2)}) %collective-permute-start) | collective-permute-done | bytes 524320 | tf_op jit(solution)/shard_map/ppermute | solution.py:125
  38.6 0.1 broadcast_select_fusion.1
  38.7 1.2 pad_maximum_fusion
  39.9 0.0 all-gather.11.cloned.1.call-update
  39.9 0.0 all-gather.9.cloned.1.call-start
  39.9 0.4 copy-done.1
  40.3 0.1 copy.8
  40.4 19.5 %all_to_all.19 = bf16[256,8,256]{2,0,1:T(8,128)(2,1)} all-to-all(bf16[256,8,256]{2,0,1:T(8,128)(2,1)S(1)} %bitcast.19), channel_id=1, replica_groups=mesh['width'=4,'row'=4,'src'=8] {'src'}, dimensions={1} | all-to-all | bytes 2097152 | tf_op jit(solution)/shard_map/all_to_all | solution.py:130
  59.9 0.0 all-gather.9.cloned.1.call-update
  59.9 0.0 reduce-scatter.2.cloned.1.call-start
  59.9 0.0 all-gather.13.cloned.1.call-done
  60.0 21.4 %all-gather.7.cloned.1.call-done.v = bf16[1024,1024]{1,0:T(8,128)(2,1)} async-done(((bf16[128,1024]{1,0:T(8,128)(2,1)}), bf16[1024,1024]{1,0:T(8,128)(2,1)}) %all-gather.7.cloned.1.call-update) | async-done | bytes 2097168 | tf_op jit(solution)/shard_map/all_gather | solution.py:129
  81.3 50.1 %all-gather.11.cloned.1.call-done = bf16[1024,2048]{1,0:T(8,128)(2,1)} async-done(((bf16[256,2048]{1,0:T(8,128)(2,1)}), bf16[1024,2048]{1,0:T(8,128)(2,1)}) %all-gather.11.cloned.1.call-update) | async-done | bytes 4194320 | tf_op jit(solution)/shard_map/all_gather | solution.py:127
  131.4 48.1 %all-gather.9.cloned.1.call-done.o = bf16[8192,256]{1,0:T(8,128)(2,1)} async-done(((bf16[2048,256]{1,0:T(8,128)(2,1)}), bf16[8192,256]{1,0:T(8,128)(2,1)}) %all-gather.9.cloned.1.call-update) | async-done | bytes 4194320 | tf_op jit(solution)/shard_map/all_gather | solution.py:131
  179.5 60.2 %shard_map.46 = f32[2,1024,128]{2,1,0:T(8,128)} custom-call(bf16[4,256,2048]{2,1,0:T(8,128)(2,1)} %bitcast.17, bf16[4,1024,256]{2,1,0:T(8,128)(2,1)} %bitcast.20, bf16[1024,1024]{1,0:T(8,128)(2,1)} %all-gather.7.cloned.1.call-done.v, bf16[8192,256]{1,0:T(8,128)(2,1)} %all-gather.9.cloned.1.call-done.o), custom_call_target="tpu_custom_call" | custom-call | tf_op jit(solution)/shard_map/pallas_call | solution.py:114
  239.7 0.0 reduce-scatter.2.cloned.1.call-update
  239.7 0.1 add_multiply_fusion
  239.8 78.5 %reduce-scatter.2.cloned.1.call-done = f32[2,32,128]{2,1,0:T(8,128)} async-done(((f32[2,1024,128]{2,1,0:T(8,128)}), f32[2,32,128]{2,1,0:T(8,128)}) %reduce-scatter.2.cloned.1.call-update) | async-done | bytes 32784 | tf_op jit(solution)/shard_map/reduce_scatter | solution.py:133
  318.3 0.8 reduce_sum.9
  319.1 61.2 %psum.7 = f32[2,128]{1,0:T(2,128)S(1)} all-reduce(f32[2,128]{1,0:T(2,128)S(1)} %reduce_sum.9), channel_id=1, replica_groups=mesh['width'=4,'row'=4,'src'=8] {'src','width'}, use_global_device_ids=true, to_apply=%region_2.3 | all-reduce | flops 256 | bytes 2048 | tf_op jit(solution)/shard_map/psum | solution.py:134
  380.3 0.1 convert_divide_fusion
  380.4 0.8 multiply_bitcast_fusion
  381.1 0.3 collective-permute-start.1
  381.5 3.6 collective-permute-done.1
  385.0 0.6 pad_maximum_fusion.1
  (6 shorter events, 0.0 us)
Async XLA Ops:
  6.5 32.1 %copy-start = (bf16[256,2048]{1,0:T(8,128)(2,1)S(1)}, bf16[256,2048]{1,0:T(8,128)(2,1)}, u32[]{:S(2)}) copy-start(bf16[256,2048]{1,0:T(8,128)(2,1)} %param.4) | copy-start | bytes 3145732
  6.5 53.4 %all-gather.13.cloned.1.call-start = ((), (), s32[]{:S(2)}) async-start(), calls=%async_computation.6 | async-start | bytes 2621440 | tf_op jit(solution)/shard_map/all_gather | solution.py:128
  21.9 59.4 %all-gather.7.cloned.1.call-start = ((), (), s32[]{:S(2)}) async-start(), calls=%async_computation.2 | async-start | bytes 2359296 | tf_op jit(solution)/shard_map/all_gather | solution.py:129
  22.7 108.7 %all-gather.11.cloned.1.call-start = ((), (), s32[]{:S(2)}) async-start(), calls=%async_computation.5 | async-start | bytes 5242880 | tf_op jit(solution)/shard_map/all_gather | solution.py:127
  23.8 14.8 %collective-permute-start = (bf16[128,2048]{1,0:T(8,128)(2,1)S(1)}, bf16[128,2048]{1,0:T(8,128)(2,1)S(1)}, u32[]{:S(2)}, u32[]{:S(2)}) collective-permute-start(bf16[128,2048]{1,0:T(8,128)(2,1)S(1)} %slice.15), channel_id=1, source_target_pairs={{0,24},{24,0},{8,16},{16,8},{1,25},{25,1},{9,17},{17,9},{2,26},{26... | collective-permute-start | bytes 1572872 | tf_op jit(solution)/shard_map/ppermute | solution.py:125
  38.7 1.6 copy-start.1
  39.9 139.6 %all-gather.9.cloned.1.call-start = ((), (), s32[]{:S(2)}) async-start(), calls=%async_computation.3 | async-start | bytes 5242880 | tf_op jit(solution)/shard_map/all_gather | solution.py:131
  59.9 258.4 %reduce-scatter.2.cloned.1.call-start = ((), (), s32[]{:S(2)}) async-start(), calls=%async_computation.4 | async-start | bytes 1081344 | tf_op jit(solution)/shard_map/reduce_scatter | solution.py:133
  381.1 3.9 collective-permute-start.1
Sparse Core Ops, SparseCore 0:
  22.1 32.0 all-gather.12
  55.9 25.3 all-gather.6
  83.0 48.3 all-gather.10
  132.9 46.5 all-gather.8
  239.8 78.4 reduce-scatter.1

commit v2 on v1

--- a/solution.py
+++ b/solution.py
@@ -25,7 +25,7 @@
         def block(jb, diag):
             for hp in range(8):
                 kk = k[zc, pl.ds(pl.multiple_of(jb * 128, 128), 128), (hp // 4) * 128:(hp // 4 + 1) * 128]
-                qq = jnp.concatenate([q[zc, slot * 128:(slot + 1) * 128, (2 * hp + a) * 128:(2 * hp + a + 1) * 128] for a in (0, 1)], axis=0)
+                qq = jnp.concatenate([q[zc, slot, :, (2 * hp + a) * 128:(2 * hp + a + 1) * 128] for a in (0, 1)], axis=0)
                 s = lax.dot_general(kk, qq, (((1,), (1,)), ((), ())), preferred_element_type=F32)
                 if diag:
                     s = jnp.where(jl <= il, s, NEG)
@@ -69,7 +69,7 @@
             vvs = [v[pl.ds(pl.multiple_of(jb * 128, 128), 128), pl.ds(pl.multiple_of(g * 256 + b * 128, 128), 128)] for b in (0, 1)]
             for hh in range(16):
                 h = g * 16 + hh
-                oo = o[pl.ds(pl.multiple_of(h * 128, 128), 128), :]
+                oo = jnp.concatenate([o[a, pl.ds(pl.multiple_of(h * 128, 128), 128), :] for a in (0, 1)], axis=1)
                 x = jnp.dot(vvs[hh // 8], oo, preferred_element_type=F32)
                 for a in (0, 1):
                     IM[a, pl.ds(h, 128, stride=IS), :] = x[:, a * 128:(a + 1) * 128]
@@ -116,28 +116,258 @@
         compiler_params=pltpu.CompilerParams(vmem_limit_bytes=62 * 2**20))(q, k, v, o)
 
 
-PARTNER = [(0, 3), (3, 0), (1, 2), (2, 1)]
+MESH = pl.DeviceIdType.MESH
+
+
+class Links:
+    def __init__(self, send, recv, at=None):
+        self.send, self.recv, self.n, self.at = send, recv, 0, at
+
+    def to(self, source, target, **where):
+        i = self.n
+        self.n += 1
+        return pltpu.make_async_remote_copy(src_ref=source, dst_ref=target, send_sem=self.send.at[i], recv_sem=self.recv.at[i],
+                                            device_id={**self.at, **where}, device_id_type=MESH)
+
+
+def start_all(copies):
+    for cp in copies:
+        cp.start()
+    return copies
+
+
+def gather_kernel(q, k, v, o, Q, K, V, OC, send, recv, local):
+    z, y, s = lax.axis_index("width"), lax.axis_index("row"), lax.axis_index("src")
+    x, c = s // 2, s % 2
+    at = {"width": z, "row": y, "src": s}
+    zu, zd, zf = (z + 1) % 4, (z + 3) % 4, (z + 2) % 4
+    yu, yd, yf = (y + 1) % 4, (y + 3) % 4, (y + 2) % 4
+    xu, xd, xf = (x + 1) % 4, (x + 3) % 4, (x + 2) % 4
+    su, sd, sib = xu * 2 + c, xd * 2 + c, x * 2 + 1 - c
+    partner = 3 - y
+    tslot = y // 2
+
+    barrier = pltpu.get_barrier_semaphore()
+
+    def greet(**where):
+        pl.semaphore_signal(barrier, inc=1, device_id={**at, **where}, device_id_type=MESH)
+
+    greet(width=zu)
+    greet(width=zd)
+    greet(row=yu)
+    greet(row=yd)
+    for d in range(1, 8):
+        greet(src=(s + d) % 8)
+    pl.semaphore_wait(barrier, 11)
+
+    links = Links(send, recv, at)
+    to = links.to
+    mine = pl.ds(s * 128, 128)
+
+    def ksl(a):
+        return pl.ds(a * 128, 128)
+
+    swap = to(q.at[pl.ds(128, 128), :], Q.at[z, c], row=partner)
+    loc_q = pltpu.make_async_copy(q.at[pl.ds(0, 128), :], Q.at[z, c], local.at[0])
+
+    @pl.when(c == tslot)
+    def _():
+        swap.start()
+        loc_q.start()
+
+    locs = [pltpu.make_async_copy(k, K.at[z, mine, :], local.at[1]),
+            pltpu.make_async_copy(v, V.at[mine, :], local.at[2])]
+    locs += [pltpu.make_async_copy(o.at[:, pl.ds(s * 256 + ch * 128, 128)], OC.at[ch, pl.ds((y * 8 + s) * 256, 256), :], local.at[3 + ch]) for ch in (0, 1)]
+    start_all(locs)
+    kz = start_all([to(k, K.at[z, mine, :], width=w) for w in (zu, zd)])
+    ox = []
+    for ch in (0, 1):
+        ox.append(start_all([to(o.at[:, pl.ds(((s + d) % 8) * 256 + ch * 128, 128)], OC.at[ch, pl.ds((y * 8 + s) * 256, 256), :], src=(s + d) % 8) for d in range(1, 8)]))
+        if ch == 0:
+            vx = start_all([to(v, V.at[mine, :], src=w) for w in (su, sd, sib)])
+
+    @pl.when(c == tslot)
+    def _():
+        loc_q.wait()
+
+    @pl.when(c != tslot)
+    def _():
+        swap.wait_recv()
+
+    def qring(ref_of):
+        return start_all([to(ref_of, ref_of, width=w) for w in (zu, zd)])
+
+    qz = qring(Q.at[z, c])
+    qs = start_all([to(Q.at[z, c], Q.at[z, c], src=sib)])
+
+    def part(ref, lo, n):
+        return ref.at[pl.ds(lo, n)]
+
+    kz[0].wait_recv()
+    ks = pl.ds(s * 128, 64)
+    ks2 = pl.ds(s * 128 + 64, 64)
+    kf = [to(K.at[zd, ks, :], K.at[zd, ks, :], width=zu), to(K.at[zu, ks2, :], K.at[zu, ks2, :], width=zd)]
+    kf[0].start()
+    kz[1].wait_recv()
+    kf[1].start()
+    for cp in locs:
+        cp.wait()
+    for cp in kf:
+        cp.wait_recv()
+    kx = start_all([to(K.at[:, mine, :], K.at[:, mine, :], src=w) for w in (su, sd, sib)])
+
+    def rows(a):
+        return pl.ds((a * 2 + c) * 128, 128)
+
+    def vhalf(a, h):
+        return V.at[pl.ds((a * 2 + c) * 128 + h * 64, 64), :]
+
+    def khalf(a, h):
+        return K.at[pl.ds(h * 2, 2), rows(a), :]
+
+    def onward(first, half, whole):
+        first[0].wait_recv()
+        f0 = to(half(xd, 0), half(xd, 0), src=su)
+        f0.start()
+        g0 = to(whole(xd), whole(xd), src=sib)
+        g0.start()
+        first[1].wait_recv()
+        f1 = to(half(xu, 1), half(xu, 1), src=sd)
+        f1.start()
+        g1 = to(whole(xu), whole(xu), src=sib)
+        g1.start()
+        return [f0, f1], [g0, g1]
+
+    vf, vg = onward(vx, vhalf, lambda a: V.at[rows(a), :])
+    kxf, kg = onward(kx, khalf, lambda a: K.at[:, rows(a), :])
+
+    def orows(ch, a, lo, n):
+        return OC.at[ch, pl.ds(a * 2048 + lo, n), :]
+
+    oy = []
+    for ch in (0, 1):
+        for cp in ox[ch]:
+            cp.wait_recv()
+        oy.append(start_all([to(orows(ch, y, 0, 2048), orows(ch, y, 0, 2048), row=w) for w in (yu, yd)]))
+        if ch == 0:
+            qz[0].wait_recv()
+            qf = [to(Q.at[zd, c, pl.ds(0, 64)], Q.at[zd, c, pl.ds(0, 64)], width=zu),
+                  to(Q.at[zu, c, pl.ds(64, 64)], Q.at[zu, c, pl.ds(64, 64)], width=zd)]
+            qf[0].start()
+            qs += start_all([to(Q.at[zd, c], Q.at[zd, c], src=sib)])
+            qz[1].wait_recv()
+            qf[1].start()
+            qs += start_all([to(Q.at[zu, c], Q.at[zu, c], src=sib)])
+            for cp in vf + kxf:
+                cp.wait_recv()
+            vg += start_all([to(V.at[rows(xf), :], V.at[rows(xf), :], src=sib)])
+            kg += start_all([to(K.at[:, rows(xf), :], K.at[:, rows(xf), :], src=sib)])
+    of = []
+    for ch in (0, 1):
+        oy[ch][0].wait_recv()
+        a = to(orows(ch, yd, 0, 1024), orows(ch, yd, 0, 1024), row=yu)
+        a.start()
+        oy[ch][1].wait_recv()
+        b = to(orows(ch, yu, 1024, 1024), orows(ch, yu, 1024, 1024), row=yd)
+        b.start()
+        of += [a, b]
+        if ch == 0:
+            for cp in qf:
+                cp.wait_recv()
+            qs += start_all([to(Q.at[zf, c], Q.at[zf, c], src=sib)])
+
+    for cp in [vx[2], kx[2]] + vg + kg + qs + of:
+        cp.wait_recv()
+    for cp in kz + ox[0] + ox[1] + vx + qz + qs + kf + kx + vf + vg + kxf + kg + qf + oy[0] + oy[1] + of:
+        cp.wait_send()
+
+    @pl.when(c == tslot)
+    def _():
+        swap.wait_send()
+
+
+def gather(q, k, v, o):
+    vm = pl.BlockSpec(memory_space=pltpu.VMEM)
+    hb = pl.BlockSpec(memory_space=pl.ANY)
+    return pl.pallas_call(gather_kernel,
+        out_shape=[jax.ShapeDtypeStruct((4, 2, 128, 2048), BF), jax.ShapeDtypeStruct((4, 1024, 256), BF),
+                   jax.ShapeDtypeStruct((1024, 1024), BF), jax.ShapeDtypeStruct((2, 8192, 128), BF)],
+        in_specs=[hb] * 4, out_specs=[vm] * 4,
+        scratch_shapes=[pltpu.SemaphoreType.DMA((64,)), pltpu.SemaphoreType.DMA((64,)), pltpu.SemaphoreType.DMA((8,))],
+        compiler_params=pltpu.CompilerParams(collective_id=0, has_side_effects=True, vmem_limit_bytes=40 * 2**20))(q, k, v, o)
+
+
+def finish_kernel(part, out, RB, TB, TL, NB, send, recv, tsend, trecv, wsem):
+    z, y, s = lax.axis_index("width"), lax.axis_index("row"), lax.axis_index("src")
+    me = s * 4 + z
+    at = {"width": z, "row": y, "src": s}
+    partner = 3 - y
+    barrier = pltpu.get_barrier_semaphore()
+
+    def peer(d):
+        n = (me + d) % 32
+        return n, {"width": n % 4, "row": y, "src": n // 4}
+
+    def greet(d, c):
+        pl.semaphore_signal(barrier, inc=1, device_id=peer(d)[1], device_id_type=MESH)
+        return c
+    lax.fori_loop(1, 32, greet, 0)
+    pl.semaphore_signal(barrier, inc=1, device_id={**at, "row": partner}, device_id_type=MESH)
+    t = jnp.concatenate([jnp.sum(part[a].reshape(128, 8, 128), axis=0) for a in (0, 1)], axis=0)
+    TL[...] = t
+    TB[me] = t
+    pl.semaphore_wait(barrier, 32)
+
+    def block_to(d):
+        n, where = peer(d)
+        return pltpu.make_async_remote_copy(part.at[:, pl.ds(n * 32, 32), :], RB.at[me], send.at[d], recv.at[d], device_id=where, device_id_type=MESH)
+
+    def total_to(d):
+        n, where = peer(d)
+        return pltpu.make_async_remote_copy(TL, TB.at[me], tsend.at[d], trecv.at[d], device_id=where, device_id_type=MESH)
+
+    def begin(d, c):
+        block_to(d).start()
+        total_to(d).start()
+        return c
+    lax.fori_loop(1, 32, begin, 0)
+    RB[me] = part[:, pl.ds(pl.multiple_of(me * 32, 32), 32), :]
+
+    def finish(d, c):
+        block_to(d).wait()
+        total_to(d).wait()
+        return c
+    lax.fori_loop(1, 32, finish, 0)
+    norms = jnp.sum(RB[...], axis=0)
+    tb = jnp.sum(TB[...], axis=0)
+    p = pair_of(y)
+    share = []
+    for a, ib in ((0, p), (1, 7 - p)):
+        total = jnp.sum(tb[8 * a:8 * a + 8], axis=0, keepdims=True)
+        pos = (ib * 128 + 1 + lax.broadcasted_iota(jnp.int32, (1, 128), 1)).astype(F32)
+        share.append(jnp.transpose(norms[a] * (pos / total)))
+    low = y < 2
+    kept, other = jnp.where(low, share[0], share[1]), jnp.where(low, share[1], share[0])
+    out[0:128, :] = kept
+    NB[...] = other
+    cp = pltpu.make_async_remote_copy(NB, out.at[pl.ds(128, 128), :], wsem.at[0], wsem.at[1], device_id={**at, "row": partner}, device_id_type=MESH)
+    cp.start()
+    cp.wait()
+
+
+def finish(part):
+    vm = pl.BlockSpec(memory_space=pltpu.VMEM)
+    D = pltpu.SemaphoreType.DMA((32,))
+    return pl.pallas_call(finish_kernel, out_shape=jax.ShapeDtypeStruct((256, 32), F32),
+        in_specs=[vm], out_specs=vm,
+        scratch_shapes=[pltpu.VMEM((32, 2, 32, 128), F32), pltpu.VMEM((32, 16, 128), F32), pltpu.VMEM((16, 128), F32), pltpu.VMEM((128, 32), F32),
+                        D, D, D, D, pltpu.SemaphoreType.DMA((2,))],
+        compiler_params=pltpu.CompilerParams(collective_id=1, has_side_effects=True))(part)
 
 
 def body(query_rows, key_rows, value_rows, out_proj):
-    row = lax.axis_index("row")
-    low = row < 2
-    kept, other = query_rows[:128], lax.ppermute(query_rows[128:], "row", PARTNER)
-    small, big = jnp.where(low, kept, other), jnp.where(low, other, kept)
-    q = lax.all_gather(jnp.concatenate([small, big], axis=0), "width")
-    k = lax.all_gather(lax.all_gather(key_rows, "src", tiled=True), "width")
-    v = lax.all_gather(value_rows, "src", tiled=True)
-    o = lax.all_to_all(out_proj, "src", 1, 0, tiled=True)
-    o = lax.all_gather(o, "row", tiled=True)
-    part = contributions(q, k, v, o)
-    norms = lax.psum_scatter(part, ("src", "width"), scatter_dimension=1, tiled=True)
-    totals = lax.psum(jnp.sum(norms, axis=1), ("src", "width"))
-    p = pair_of(row)
-    pos = jnp.stack([p, 7 - p])[:, None] * 128 + jnp.arange(1, 129, dtype=jnp.int32)[None, :]
-    share = norms * (pos.astype(F32) / totals)[:, None, :]
-    share = share.transpose(0, 2, 1)
-    kept, other = jnp.where(low, share[0], share[1]), jnp.where(low, share[1], share[0])
-    return jnp.concatenate([kept, lax.ppermute(other, "row", PARTNER)], axis=0)
+    q, k, v, o = gather(query_rows, key_rows, value_rows, out_proj)
+    return finish(contributions(q, k, v, o))
 
 
 def solution(mesh):

time: 398 us -> 170 us (0.43)
  waiting for transfers between devices: 217 us -> 0 us
  Pallas kernels: 60.2 us -> 157 us
  blocking collectives: 96.1 us -> 0 us
  between operations: 13.2 us -> 0.03 us
  local copies, waits for them, and re-layouts: 1.52 us -> 10.5 us
    all_gather x4 -> x0, waiting for transfers between devices: 120 us -> none  [the longest x1 50.1 us: body(): q = lax.all_gather(jnp.concatenate([small, big], axis=0), 'width')]
    pallas_call x0 -> x2, Pallas kernels: none -> 96.8 us  [the longest x1 64.9 us: gather(): pl.pallas_call(gather_kernel, out_shape=[jax.ShapeDtypeStruct((4, 2, 128,...]
    reduce_scatter x1 -> x0, waiting for transfers between devices: 78.5 us -> none  [body(): lax.psum_scatter(part, ('src', 'width'), scatter_dimension=1, tiled=True)]
    psum x1 -> x0, blocking collectives: 61.2 us -> none  [body(): totals = lax.psum(jnp.sum(norms, axis=1), ('src', 'width'))]
    all_to_all x1 -> x0, blocking collectives: 19.5 us -> none  [body(): o = lax.all_to_all(out_proj, 'src', 1, 0, tiled=True)]
    ppermute x2 -> x0, waiting for transfers between devices: 18.2 us -> none  [the longest x1 14.7 us: body(): lax.ppermute(query_rows[128:], 'row', PARTNER)]
    all_gather x1 -> x0, blocking collectives: 15.4 us -> none  [body(): k = lax.all_gather(lax.all_gather(key_rows, 'src', tiled=True), 'width')]
    unnamed x4 -> x14, local copies, waits for them, and re-layouts: 0.37 us -> 8.9 us
  transfers between devices with their start and end apart: 7 -> 0, of which waited for: 6 -> 0; matrix products, arithmetic and copies ran while one was open for 1% -> 0% of each run, Pallas kernels for 0% -> 0%
where the time goes in v2:
time: 170 us; the launch traced here: 168 us
  Pallas kernels  157 us (92%)
  local copies, waits for them, and re-layouts  10.5 us (6%)
    pallas_call x1, Pallas kernels, gather(): pl.pallas_call(gather_kernel, out_shape=[jax.ShapeDtypeStruct((4, 2, 128,...  64.9 us
    pallas_call x1, Pallas kernels, contributions(): pl.pallas_call(kernel_b, out_shape=jax.ShapeDtypeStruct((2, 1024, 128), F...  60.2 us
    pallas_call x1, Pallas kernels, finish(): pl.pallas_call(finish_kernel, out_shape=jax.ShapeDtypeStruct((256, 32), F...  31.9 us
    unnamed x14, local copies, waits for them, and re-layouts  8.9 us

profile of v2, /device:TPU:25, one launch (start us, length us, event | category | flops | bytes accessed | tf_op | source)
XLA Modules:
  0.0 167.5 jit_solution(16313516422828309758)
XLA Ops:
  0.0 0.0 copy-start.3
  0.0 1.2 copy-done.3
  1.2 0.0 copy-start.4
  1.2 1.2 copy-done.4
  2.5 0.0 copy-start.5
  2.5 0.9 copy-done.5
  3.4 0.0 copy-start.6
  3.4 0.8 copy-done.6
  4.2 64.9 %shard_map.46 = (bf16[4,2,128,2048]{3,2,1,0:T(8,128)(2,1)S(1)}, bf16[4,1024,256]{2,1,0:T(8,128)(2,1)S(1)}, bf16[1024,1024]{1,0:T(8,128)(2,1)S(1)}, bf16[2,8192,128]{2,1,0:T(8,128)(2,1)}) custom-call(bf16[256,2048]{1,0:T(8,128)(2,1)S(1)} %copy-done.3, bf16[128,256]{1,0:T(8,128)(2,1)S(1)} %copy-done.6, bf16[128,1024]{1,0:T(8,128)(2,1)S(1)} %copy-done.5, ...), custom_call_target="tpu_custom_call" | custom-call | tf_op jit(solution)/shard_map/pallas_call | solution.py:292
  69.2 0.0 copy-start
  69.2 2.0 %copy-done = bf16[4,2,128,2048]{3,2,1,0:T(8,128)(2,1)} copy-done((bf16[4,2,128,2048]{3,2,1,0:T(8,128)(2,1)}, bf16[4,2,128,2048]{3,2,1,0:T(8,128)(2,1)S(1)}, u32[]{:S(2)}) %copy-start) | copy-done | bytes 4194328
  71.2 0.0 copy-start.1
  71.2 1.4 copy-done.1
  72.5 0.0 copy-start.2
  72.5 1.3 copy-done.2
  73.9 60.2 %shard_map.47.part = f32[2,1024,128]{2,1,0:T(8,128)} custom-call(bf16[4,2,128,2048]{3,2,1,0:T(8,128)(2,1)} %copy-done, bf16[4,1024,256]{2,1,0:T(8,128)(2,1)} %copy-done.1, bf16[1024,1024]{1,0:T(8,128)(2,1)} %copy-done.2, bf16[2,8192,128]{2,1,0:T(8,128)(2,1)} %get-tuple-element.12.o), custom_call_target="tpu_custom_call" | custom-call | tf_op jit(solution)/shard_map/pallas_call | solution.py:114
  134.1 31.9 %shard_map.48 = f32[256,32]{1,0:T(8,128)} custom-call(f32[2,1024,128]{2,1,0:T(8,128)} %shard_map.47.part), custom_call_target="tpu_custom_call" | custom-call | tf_op jit(solution)/shard_map/pallas_call | solution.py:361
  165.9 1.6 copy.5
Async XLA Ops:
  0.0 1.2 copy-start.3
  1.2 1.2 copy-start.4
  2.5 0.9 copy-start.5
  3.4 0.8 copy-start.6
  69.2 2.0 %copy-start = (bf16[4,2,128,2048]{3,2,1,0:T(8,128)(2,1)}, bf16[4,2,128,2048]{3,2,1,0:T(8,128)(2,1)S(1)}, u32[]{:S(2)}) copy-start(bf16[4,2,128,2048]{3,2,1,0:T(8,128)(2,1)S(1)} %get-tuple-element.9.q) | copy-start | bytes 12582916
  71.2 1.4 copy-start.1
  72.5 1.3 copy-start.2

commit v3 on v1

v3 whole, which is shorter than its diff:
```python
import math
import jax, jax.numpy as jnp
from jax import lax
from jax.experimental import pallas as pl
from jax.experimental.pallas import tpu as pltpu
from jax.sharding import PartitionSpec as PS_
C2 = math.log2(math.e) / math.sqrt(128.0)
F32, BF = jnp.float32, jnp.bfloat16
NEG = -1e30
PS, IS = 17, 65

def pair_of(y):
    return jnp.where(y == 0, 0, jnp.where(y == 3, 1, y + 1))

SCR = [pltpu.VMEM((8, 128 * PS, 128), F32), pltpu.VMEM((9, 128, 64, 128), BF),
       pltpu.VMEM((8, 16, 128), F32), pltpu.VMEM((8, 16, 128), F32), pltpu.VMEM((8, 16, 128), F32),
       pltpu.VMEM((2, 128 * IS, 128), F32)]


MESH = pl.DeviceIdType.MESH


class Links:
    def __init__(self, send, recv, at=None):
        self.send, self.recv, self.n, self.at = send, recv, 0, at

    def to(self, source, target, **where):
        i = self.n
        self.n += 1
        return pltpu.make_async_remote_copy(src_ref=source, dst_ref=target, send_sem=self.send.at[i], recv_sem=self.recv.at[i],
                                            device_id={**self.at, **where}, device_id_type=MESH)


def layer_kernel(qi, ki, vi, oi, out, Q, K, V, OC, P, W, MS, LS, FS, IM, part, RB, TB, TL, NB,
                 send, recv, local, rsend, rrecv, tsend, trecv, wsem):
    z, y, s = lax.axis_index("width"), lax.axis_index("row"), lax.axis_index("src")
    x, c = s // 2, s % 2
    me = s * 4 + z
    p = pair_of(y)
    big = 7 - p
    at = {"width": z, "row": y, "src": s}
    zu, zd, zf = (z + 1) % 4, (z + 3) % 4, (z + 2) % 4
    yu, yd = (y + 1) % 4, (y + 3) % 4
    xu, xd, xf = (x + 1) % 4, (x + 3) % 4, (x + 2) % 4
    su, sd, sib = xu * 2 + c, xd * 2 + c, x * 2 + 1 - c
    partner = 3 - y
    tslot = y // 2

    barrier = pltpu.get_barrier_semaphore()

    def peer(n):
        return {"width": n % 4, "row": y, "src": n // 4}

    def greet(d, carry):
        pl.semaphore_signal(barrier, inc=1, device_id=peer((me + d) % 32), device_id_type=MESH)
        return carry
    lax.fori_loop(1, 32, greet, 0)
    for r in (yu, yd):
        pl.semaphore_signal(barrier, inc=1, device_id={**at, "row": r}, device_id_type=MESH)
    pl.semaphore_wait(barrier, 33)

    links = Links(send, recv, at)
    to = links.to
    mine = pl.ds(s * 128, 128)

    def rows(a):
        return pl.ds((a * 2 + c) * 128, 128)

    def oblock(a, b, ch):
        return OC.at[ch, pl.ds((a * 8 + b) * 256, 256), :]

    def orows(ch, a, lo, n):
        return OC.at[ch, pl.ds(a * 2048 + lo, n), :]

    def both(ref, *wheres):
        return [to(ref, ref, **w) for w in wheres]

    ups = [dict(src=su), dict(src=sd), dict(src=sib)]
    swap = to(qi.at[pl.ds(128, 128), :], Q.at[z, c], row=partner)
    loc_q = pltpu.make_async_copy(qi.at[pl.ds(0, 128), :], Q.at[z, c], local.at[0])
    locs = [pltpu.make_async_copy(ki, K.at[z, mine, :], local.at[1]), pltpu.make_async_copy(vi, V.at[mine, :], local.at[2])]
    locs += [pltpu.make_async_copy(oi.at[:, pl.ds(s * 256 + ch * 128, 128)], oblock(y, s, ch), local.at[3 + ch]) for ch in (0, 1)]
    kz = [to(ki, K.at[z, mine, :], width=w) for w in (zu, zd)]
    ox = [[to(oi.at[:, pl.ds(((s + d) % 8) * 256 + ch * 128, 128)], oblock(y, s, ch), src=(s + d) % 8) for d in range(1, 8)] for ch in (0, 1)]
    vx = [to(vi, V.at[mine, :], **w) for w in ups]
    qz = both(Q.at[z, c], dict(width=zu), dict(width=zd))
    qs = [both(Q.at[a, c], dict(src=sib))[0] for a in (z, zd, zu, zf)]
    lo, hi = pl.ds(s * 128, 64), pl.ds(s * 128 + 64, 64)
    kf = both(K.at[zd, lo, :], dict(width=zu)) + both(K.at[zu, hi, :], dict(width=zd))
    kx = both(K.at[:, mine, :], *ups)
    kxf = both(K.at[pl.ds(0, 2), rows(xd), :], dict(src=su)) + both(K.at[pl.ds(2, 2), rows(xu), :], dict(src=sd))
    kg = [both(K.at[:, rows(a), :], dict(src=sib))[0] for a in (xd, xu, xf)]
    vf = both(V.at[pl.ds((xd * 2 + c) * 128, 64), :], dict(src=su)) + both(V.at[pl.ds((xu * 2 + c) * 128 + 64, 64), :], dict(src=sd))
    vg = [both(V.at[rows(a), :], dict(src=sib))[0] for a in (xd, xu, xf)]
    qf = both(Q.at[zd, c, pl.ds(0, 64)], dict(width=zu)) + both(Q.at[zu, c, pl.ds(64, 64)], dict(width=zd))
    oy = [both(orows(ch, y, 0, 2048), dict(row=yu), dict(row=yd)) for ch in (0, 1)]
    of = [both(orows(ch, yd, 0, 1024), dict(row=yu)) + both(orows(ch, yu, 1024, 1024), dict(row=yd)) for ch in (0, 1)]

    def start(*copies):
        for cp in copies:
            cp.start()

    def arrived(*copies):
        for cp in copies:
            cp.wait_recv()

    start(*locs, *kz)

    @pl.when(c == tslot)
    def _():
        loc_q.start()
        swap.start()
    start(*ox[0])

    @pl.when(c == tslot)
    def _():
        loc_q.wait()
        start(*qz, qs[0])
    arrived(kz[0])
    start(kf[0])
    arrived(kz[1])
    start(kf[1])
    for cp in locs:
        cp.wait()
    arrived(*kf)
    start(*kx)

    @pl.when(c != tslot)
    def _():
        arrived(swap)
        start(*qz, qs[0])
    arrived(kx[0])
    start(kxf[0], kg[0])
    arrived(kx[1])
    start(kxf[1], kg[1])
    arrived(*ox[0])
    start(*oy[0])
    start(*ox[1], *vx)
    arrived(*kxf)
    start(kg[2])
    part[...] = jnp.zeros(part.shape, F32)
    arrived(kx[2], *kg, qs[0])

    jl = lax.broadcasted_iota(jnp.int32, (128, 256), 0)
    il = lax.broadcasted_iota(jnp.int32, (128, 256), 1) % 128

    def scores(zc, slot, ib, base):
        MS[...] = jnp.full(MS.shape, NEG, F32)
        LS[...] = jnp.zeros(LS.shape, F32)

        def block(jb, diag):
            for hp in range(8):
                kk = K[zc, pl.ds(pl.multiple_of(jb * 128, 128), 128), (hp // 4) * 128:(hp // 4 + 1) * 128]
                qq = jnp.concatenate([Q[zc, slot, :, (2 * hp + a) * 128:(2 * hp + a + 1) * 128] for a in (0, 1)], axis=0)
                sc = lax.dot_general(kk, qq, (((1,), (1,)), ((), ())), preferred_element_type=F32)
                if diag:
                    sc = jnp.where(jl <= il, sc, NEG)
                m = jnp.max(sc, axis=0, keepdims=True)
                e = jnp.exp2((sc - m) * C2)
                l = jnp.sum(e, axis=0, keepdims=True)
                for a in (0, 1):
                    lanes = slice(a * 128, (a + 1) * 128)
                    P[jb, pl.ds(2 * hp + a, 128, stride=PS), :] = e[:, lanes]
                    MS[jb, 2 * hp + a:2 * hp + a + 1, :] = m[:, lanes]
                    LS[jb, 2 * hp + a:2 * hp + a + 1, :] = l[:, lanes]

        def plain(jb, carry):
            block(jb, False)
            return carry
        lax.fori_loop(0, ib, plain, 0)
        block(ib, True)
        ms = MS[...]
        f = jnp.exp2((ms - jnp.max(ms, axis=0, keepdims=True)) * C2)
        total = jnp.sum(f * LS[...], axis=0, keepdims=True)
        FS[...] = f / total

        def conv(jb, carry):
            fs = FS[jb]
            for j in range(128):
                W[base + jb, j, pl.ds(pl.multiple_of(zc * 16, 16), 16), :] = (P[jb, j * PS:j * PS + 16, :] * fs).astype(BF)
            return carry
        lax.fori_loop(0, ib + 1, conv, 0)

    def zstep(d, carry):
        @pl.when(d == 1)
        def _():
            arrived(*ox[1])
            start(*oy[1])
            arrived(qz[0])
            start(qf[0], qs[1])
            arrived(qz[1])
            start(qf[1], qs[2])
            arrived(vx[0])
            start(vf[0], vg[0])
            arrived(vx[1])
            start(vf[1], vg[1])
            arrived(qs[1])

        @pl.when(d == 2)
        def _():
            arrived(oy[0][0])
            start(of[0][0])
            arrived(oy[0][1])
            start(of[0][1])
            arrived(*vf)
            start(vg[2])
            arrived(*qf)
            start(qs[3])
            arrived(qs[2])

        @pl.when(d == 3)
        def _():
            arrived(qs[3])
        zc = (z + jnp.where(d == 1, 3, jnp.where(d == 2, 1, jnp.where(d == 3, 2, 0)))) % 4
        scores(zc, 0, p, big + 1)
        scores(zc, 1, big, 0)
        return carry
    lax.fori_loop(0, 4, zstep, 0)

    arrived(oy[1][0])
    start(of[1][0])
    arrived(oy[1][1])
    start(of[1][1])
    arrived(vx[2], *vg, *of[0], *of[1])

    def block_to(n):
        return pltpu.make_async_remote_copy(part.at[:, pl.ds(n * 32, 32), :], RB.at[me], rsend.at[n], rrecv.at[me], device_id=peer(n), device_id_type=MESH)

    def block_from(n):
        return pltpu.make_async_remote_copy(part.at[:, pl.ds(n * 32, 32), :], RB.at[n], rsend.at[n], rrecv.at[n], device_id=peer(n), device_id_type=MESH)

    def total_to(d):
        return pltpu.make_async_remote_copy(TL, TB.at[me], tsend.at[d], trecv.at[d], device_id=peer((me + d) % 32), device_id_type=MESH)

    def jstep(jb, carry):
        def img(g, carry):
            vvs = [V[pl.ds(pl.multiple_of(jb * 128, 128), 128), pl.ds(pl.multiple_of(g * 256 + b * 128, 128), 128)] for b in (0, 1)]
            for hh in range(16):
                h = g * 16 + hh
                oo = jnp.concatenate([OC[a, pl.ds(pl.multiple_of(h * 128, 128), 128), :] for a in (0, 1)], axis=1)
                im = jnp.dot(vvs[hh // 8], oo, preferred_element_type=F32)
                for a in (0, 1):
                    IM[a, pl.ds(h, 128, stride=IS), :] = im[:, a * 128:(a + 1) * 128]
            return carry
        lax.fori_loop(0, 4, img, 0)

        def contrib(t, slot):
            zero = jnp.zeros((64, 128), BF)
            PU = 32

            def pairs(n, carry):
                got = []
                for u in range(PU):
                    j = n * (2 * PU) + 2 * u
                    r0 = pl.multiple_of(n * (2 * PU * IS), 8)
                    lhs = jnp.concatenate([jnp.concatenate([IM[a, pl.ds(r0 + (2 * u + b) * IS, 64), :].astype(BF) for b in (0, 1)], axis=0) for a in (0, 1)], axis=1)
                    rhs = jnp.concatenate([
                        jnp.concatenate([W[t, j], zero], axis=1),
                        jnp.concatenate([zero, W[t, j + 1]], axis=1)], axis=0)
                    cc = lax.dot_general(lhs, rhs, (((0,), (0,)), ((), ())), preferred_element_type=F32)
                    r = jnp.sum(jnp.abs(cc), axis=0, keepdims=True)
                    got += [r[:, :128], r[:, 128:]]
                for b in range(PU // 4):
                    part[slot, pl.ds(pl.multiple_of(jb * 128 + n * (2 * PU) + 8 * b, 8), 8), :] = jnp.concatenate(got[8 * b:8 * b + 8], axis=0)
                return carry
            lax.fori_loop(0, 128 // (2 * PU), pairs, 0)
        contrib(jb, 1)

        @pl.when(jb <= p)
        def _():
            contrib(big + 1 + jb, 0)
        for w in range(4):
            n = jb * 4 + w

            @pl.when(n != me)
            def _():
                block_to(n).start()
        return carry
    lax.fori_loop(0, big + 1, jstep, 0)

    tl = jnp.concatenate([jnp.sum(part[a].reshape(128, 8, 128), axis=0) for a in (0, 1)], axis=0)
    TL[...] = tl
    TB[me] = tl

    def tell(d, carry):
        total_to(d).start()
        return carry
    lax.fori_loop(1, 32, tell, 0)
    RB[me] = part[:, pl.ds(pl.multiple_of(me * 32, 32), 32), :]

    def heard(d, carry):
        total_to(d).wait()
        return carry
    lax.fori_loop(1, 32, heard, 0)
    for cp in kz + ox[0] + ox[1] + vx + qz + qs + kf + kx + vf + vg + kxf + kg + qf + oy[0] + oy[1] + of[0] + of[1]:
        cp.wait_send()

    @pl.when(c == tslot)
    def _():
        swap.wait_send()

    def sent(n, carry):
        @pl.when(n != me)
        def _():
            block_to(n).wait_send()
        return carry
    lax.fori_loop(0, (big + 1) * 4, sent, 0)

    tb = jnp.sum(TB[...], axis=0)

    def scale(a, ib):
        total = jnp.sum(tb[8 * a:8 * a + 8], axis=0, keepdims=True)
        pos = (ib * 128 + 1 + lax.broadcasted_iota(jnp.int32, (1, 128), 1)).astype(F32)
        return pos / total

    def emit(first, second):
        low = y < 2
        out[:, 0:128] = jnp.where(low, first, second)
        NB[...] = jnp.where(low, second, first)

    @pl.when(s <= big)
    def _():
        def take(n, carry):
            @pl.when(n != me)
            def _():
                block_from(n).wait_recv()
            return carry
        lax.fori_loop(0, 32, take, 0)
        norms = jnp.sum(RB[...], axis=0)
        emit(norms[0] * scale(0, p), norms[1] * scale(1, big))

    @pl.when(s > big)
    def _():
        emit(jnp.zeros((32, 128), F32), jnp.zeros((32, 128), F32))
    back = pltpu.make_async_remote_copy(NB, out.at[:, pl.ds(128, 128)], wsem.at[0], wsem.at[1], device_id={**at, "row": partner}, device_id_type=MESH)
    back.start()
    back.wait()


def body(query_rows, key_rows, value_rows, out_proj):
    hbm = pl.BlockSpec(memory_space=pl.ANY)
    D = pltpu.SemaphoreType.DMA
    out = pl.pallas_call(
        layer_kernel, out_shape=jax.ShapeDtypeStruct((32, 256), F32), in_specs=[hbm] * 4,
        out_specs=pl.BlockSpec(memory_space=pltpu.VMEM),
        scratch_shapes=[
            pltpu.VMEM((4, 2, 128, 2048), BF), pltpu.VMEM((4, 1024, 256), BF), pltpu.VMEM((1024, 1024), BF), pltpu.VMEM((2, 8192, 128), BF),
            *SCR, pltpu.VMEM((2, 1024, 128), F32), pltpu.VMEM((32, 2, 32, 128), F32), pltpu.VMEM((32, 16, 128), F32),
            pltpu.VMEM((16, 128), F32), pltpu.VMEM((32, 128), F32),
            D((64,)), D((64,)), D((8,)), D((32,)), D((32,)), D((32,)), D((32,)), D((2,))],
        compiler_params=pltpu.CompilerParams(collective_id=0, has_side_effects=True, vmem_limit_bytes=62 * 2**20),
    )(query_rows, key_rows, value_rows, out_proj)
    return out.T


def solution(mesh):
    placed = (PS_("row", "width"), PS_("src", "width"), PS_("src", None), PS_(("row", "src"), "width"))
    return jax.shard_map(
        body, mesh=mesh, in_specs=placed, out_specs=PS_("row", ("src", "width")), check_vma=False
    )
```

time: 398 us -> 119 us (0.30)
  the two profiles are of different devices: /device:TPU:25 before, /device:TPU:30 now
where the time goes in v3:
time: 119 us
  Pallas kernels  118 us (99%)
  local copies, waits for them, and re-layouts  1.38 us (1%)
    pallas_call x1, Pallas kernels, body(): pl.pallas_call(layer_kernel, out_shape=jax.ShapeDtypeStruct((32, 256), F3...  118 us

profile of v3, /device:TPU:30, one launch (start us, length us, event | category | flops | bytes accessed | tf_op | source)
XLA Modules:
  0.0 119.2 jit_solution(5273366858977289767)
XLA Ops:
  0.0 117.8 %shard_map.46 = f32[32,256]{1,0:T(8,128)} custom-call(bf16[256,2048]{1,0:T(8,128)(2,1)} %qi.1, bf16[128,256]{1,0:T(8,128)(2,1)} %ki.1, bf16[128,1024]{1,0:T(8,128)(2,1)} %vi.1, bf16[256,2048]{1,0:T(8,128)(2,1)} %oi.1), custom_call_target="tpu_custom_call" | custom-call | tf_op jit(solution)/shard_map/pallas_call | solution.py:343
  117.8 1.4 %copy.6 = f32[256,32]{0,1:T(8,128)} copy(f32[256,32]{0,1:T(8,128)} %bitcast.1) | data formatting | bytes 65536

commit v4 on v3

v4 whole, which is shorter than its diff:
```python
import math
import jax, jax.numpy as jnp
from jax import lax
from jax.experimental import pallas as pl
from jax.experimental.pallas import tpu as pltpu
from jax.sharding import PartitionSpec as PS_
C2 = math.log2(math.e) / math.sqrt(128.0)
F32, BF = jnp.float32, jnp.bfloat16
NEG = -1e30
PS, IS = 17, 65

SCR = [pltpu.VMEM((8, 128 * PS, 128), F32), pltpu.VMEM((9, 128, 64, 128), BF),
       pltpu.VMEM((8, 16, 128), F32), pltpu.VMEM((8, 16, 128), F32), pltpu.VMEM((8, 16, 128), F32),
       pltpu.VMEM((2, 128 * IS, 128), F32)]


MESH = pl.DeviceIdType.MESH


class Links:
    def __init__(self, send, recv, at=None):
        self.send, self.recv, self.n, self.at = send, recv, 0, at

    def to(self, source, target, **where):
        i = self.n
        self.n += 1
        return pltpu.make_async_remote_copy(src_ref=source, dst_ref=target, send_sem=self.send.at[i], recv_sem=self.recv.at[i],
                                            device_id={**self.at, **where}, device_id_type=MESH)


def layer_kernel(qi, ki, vi, oi, out, Q, K, V, OC, P, W, MS, LS, FS, IM, part, RB, TB, TL, NB,
                 send, recv, local, rsend, rrecv, tsend, trecv, wsend, wrecv):
    z, y, s = lax.axis_index("width"), lax.axis_index("row"), lax.axis_index("src")
    x, c = s // 2, s % 2
    me = s * 4 + z
    p = (x + y) % 4
    big = 7 - p
    at = {"width": z, "row": y, "src": s}
    zu, zd, zf = (z + 1) % 4, (z + 3) % 4, (z + 2) % 4
    yu, yd = (y + 1) % 4, (y + 3) % 4
    xu, xd = (x + 1) % 4, (x + 3) % 4
    su, sd, sib = xu * 2 + c, xd * 2 + c, x * 2 + 1 - c

    barrier = pltpu.get_barrier_semaphore()

    def peer(n):
        return {"width": n % 4, "row": (p + 4 - n // 8) % 4, "src": n // 4}

    def greet(**where):
        pl.semaphore_signal(barrier, inc=1, device_id={**at, **where}, device_id_type=MESH)

    def greet_peer(d, carry):
        greet(**peer((me + d) % 32))
        return carry
    for d in range(1, 8):
        greet(src=(s + d) % 8)
    for d in range(1, 4):
        for b in (0, 1):
            greet(row=(y + d) % 4, src=x * 2 + b)
    lax.fori_loop(1, 32, greet_peer, 0)
    pl.semaphore_wait(barrier, 44)

    links = Links(send, recv, at)
    to = links.to

    def both(ref, *wheres):
        return [to(ref, ref, **w) for w in wheres]

    rows = y * 2 + c
    pair = jnp.where(rows < 4, rows, 7 - rows)
    goal, slot_to = (pair + 4 - x) % 4, y // 2
    stays = jnp.logical_and(goal == y, slot_to == c)
    q_half = qi.at[pl.ds(c * 128, 128), :]
    move = to(q_half, Q.at[z, slot_to], row=goal, src=x * 2 + slot_to)
    keep = pltpu.make_async_copy(q_half, Q.at[z, c], local.at[0])
    v_own = vi.at[:, pl.ds(z * 256, 256)]

    def o_src(b):
        return oi.at[:, pl.ds(b * 128, 128)]

    def o_dst(ch):
        return OC.at[ch, y, pl.ds(s * 256, 256), :]
    loc_k = pltpu.make_async_copy(ki, K.at[z, x, c], local.at[1])
    loc_v = pltpu.make_async_copy(v_own, V.at[z, x, c], local.at[2])
    loc_o = [pltpu.make_async_copy(o_src(s), o_dst(0), local.at[3]), pltpu.make_async_copy(o_src(8 + y * 2 + c), o_dst(1), local.at[4])]
    kx = [to(ki, K.at[z, x, c], src=(s + d) % 8) for d in range(1, 8)]
    vx = [to(v_own, V.at[z, x, c], src=(s + d) % 8) for d in range(1, 8)]
    oa = [to(o_src((s + d) % 8), o_dst(0), src=(s + d) % 8) for d in range(1, 8)]
    ob = [to(o_src(8 + ((y + d) % 4) * 2 + (c + b) % 2), o_dst(1), row=(y + d) % 4, src=x * 2 + (c + b) % 2) for d in range(1, 4) for b in (0, 1)]
    ob += [to(o_src(8 + y * 2 + 1 - c), o_dst(1), src=sib)]
    ups, downs, other = dict(width=zu), dict(width=zd), dict(src=sib)
    kz = both(K.at[z, :, c], ups, downs)
    vz = both(V.at[z, :, c], ups, downs)
    qz = both(Q.at[z, c], ups, downs)
    kf = both(K.at[zd, pl.ds(0, 2), c], ups) + both(K.at[zu, pl.ds(2, 2), c], downs)
    vf = both(V.at[zd, pl.ds(0, 2), c], ups) + both(V.at[zu, pl.ds(2, 2), c], downs)
    qf = both(Q.at[zd, c, pl.ds(0, 64)], ups) + both(Q.at[zu, c, pl.ds(64, 64)], downs)
    kg = [both(K.at[a, :, c], other)[0] for a in (zd, zu, zf)]
    vg = [both(V.at[a, :, c], other)[0] for a in (zd, zu, zf)]
    qs = [both(Q.at[a, c], other)[0] for a in (z, zd, zu, zf)]
    oy = both(OC.at[0, y], dict(row=yu), dict(row=yd))
    oyf = both(OC.at[0, yd, pl.ds(0, 1024)], dict(row=yu)) + both(OC.at[0, yu, pl.ds(1024, 1024)], dict(row=yd))
    ow = both(OC.at[1, :, pl.ds(x * 512, 512)], dict(src=su), dict(src=sd))
    owf = both(OC.at[1, pl.ds(0, 2), pl.ds(xd * 512, 512)], dict(src=su)) + both(OC.at[1, pl.ds(2, 2), pl.ds(xu * 512, 512)], dict(src=sd))
    remote = kx + vx + oa + ob + kz + vz + qz + kf + vf + qf + kg + vg + qs + oy + oyf + ow + owf

    def start(*copies):
        for cp in copies:
            cp.start()

    def arrived(*copies):
        for cp in copies:
            cp.wait_recv()

    start(loc_k, *kx)

    @pl.when(stays)
    def _():
        keep.start()

    @pl.when(jnp.logical_not(stays))
    def _():
        move.start()
    start(*loc_o, loc_v, *oa, *ob)
    loc_k.wait()
    arrived(*kx)
    start(*kz)

    @pl.when(stays)
    def _():
        keep.wait()

    @pl.when(jnp.logical_not(stays))
    def _():
        arrived(move)
    start(qs[0], *qz, *vx)
    for cp in loc_o:
        cp.wait()
    loc_v.wait()
    part[...] = jnp.zeros(part.shape, F32)
    arrived(*oa)
    start(*oy)
    arrived(*ob)
    start(*ow)
    arrived(qs[0])

    jl = lax.broadcasted_iota(jnp.int32, (128, 256), 0)
    il = lax.broadcasted_iota(jnp.int32, (128, 256), 1) % 128

    def scores(zc, slot, ib, base):
        MS[...] = jnp.full(MS.shape, NEG, F32)
        LS[...] = jnp.zeros(LS.shape, F32)

        def block(jb, diag):
            for hp in range(8):
                kk = K[zc, jb // 2, jb % 2, :, (hp // 4) * 128:(hp // 4 + 1) * 128]
                qq = jnp.concatenate([Q[zc, slot, :, (2 * hp + a) * 128:(2 * hp + a + 1) * 128] for a in (0, 1)], axis=0)
                sc = lax.dot_general(kk, qq, (((1,), (1,)), ((), ())), preferred_element_type=F32)
                if diag:
                    sc = jnp.where(jl <= il, sc, NEG)
                m = jnp.max(sc, axis=0, keepdims=True)
                e = jnp.exp2((sc - m) * C2)
                l = jnp.sum(e, axis=0, keepdims=True)
                for a in (0, 1):
                    lanes = slice(a * 128, (a + 1) * 128)
                    P[jb, pl.ds(2 * hp + a, 128, stride=PS), :] = e[:, lanes]
                    MS[jb, 2 * hp + a:2 * hp + a + 1, :] = m[:, lanes]
                    LS[jb, 2 * hp + a:2 * hp + a + 1, :] = l[:, lanes]

        def plain(jb, carry):
            block(jb, False)
            return carry
        lax.fori_loop(0, ib, plain, 0)
        block(ib, True)
        ms = MS[...]
        f = jnp.exp2((ms - jnp.max(ms, axis=0, keepdims=True)) * C2)
        total = jnp.sum(f * LS[...], axis=0, keepdims=True)
        FS[...] = f / total

        def conv(jb, carry):
            fs = FS[jb]
            for j in range(128):
                W[base + jb, j, pl.ds(pl.multiple_of(zc * 16, 16), 16), :] = (P[jb, j * PS:j * PS + 16, :] * fs).astype(BF)
            return carry
        lax.fori_loop(0, ib + 1, conv, 0)

    def zstep(d, carry):
        @pl.when(d == 1)
        def _():
            arrived(*vx)
            start(*vz)
            for h in (0, 1):
                arrived(kz[h])
                start(kf[h], kg[h])
            for h in (0, 1):
                arrived(qz[h])
                start(qf[h], qs[1 + h])
            arrived(kg[0], qs[1])

        @pl.when(d == 2)
        def _():
            for h in (0, 1):
                arrived(oy[h])
                start(oyf[h])
            for h in (0, 1):
                arrived(ow[h])
                start(owf[h])
            for h in (0, 1):
                arrived(vz[h])
                start(vf[h], vg[h])
            arrived(kg[1], qs[2])

        @pl.when(d == 3)
        def _():
            arrived(*kf)
            start(kg[2])
            arrived(*qf)
            start(qs[3])
            arrived(kg[2], qs[3])
        zc = (z + jnp.where(d == 1, 3, jnp.where(d == 2, 1, jnp.where(d == 3, 2, 0)))) % 4
        scores(zc, 0, p, big + 1)
        scores(zc, 1, big, 0)
        return carry
    lax.fori_loop(0, 4, zstep, 0)

    arrived(*vf)
    start(vg[2])
    arrived(*vg, *oyf, *owf)

    def block_to(n):
        return pltpu.make_async_remote_copy(part.at[:, pl.ds(n * 32, 32), :], RB.at[me], rsend.at[n], rrecv.at[me], device_id=peer(n), device_id_type=MESH)

    def block_from(n):
        return pltpu.make_async_remote_copy(part.at[:, pl.ds(n * 32, 32), :], RB.at[n], rsend.at[n], rrecv.at[n], device_id=peer(n), device_id_type=MESH)

    def total_to(d):
        return pltpu.make_async_remote_copy(TL, TB.at[me], tsend.at[d], trecv.at[d], device_id=peer((me + d) % 32), device_id_type=MESH)

    turn = (x * (big + 1)) // 4

    def jstep(t, carry):
        jb = jnp.where(t + turn > big, t + turn - big - 1, t + turn)
        for h in range(64):
            vv = V[h // 16, jb // 2, jb % 2, :, (h // 8 % 2) * 128:(h // 8 % 2 + 1) * 128]
            oo = jnp.concatenate([OC[a, h // 16, (h % 16) * 128:(h % 16 + 1) * 128, :] for a in (0, 1)], axis=1)
            im = jnp.dot(vv, oo, preferred_element_type=F32)
            for a in (0, 1):
                IM[a, pl.ds(h, 128, stride=IS), :] = im[:, a * 128:(a + 1) * 128]

        def contrib(t, slot):
            zero = jnp.zeros((64, 128), BF)
            PU = 64

            def pairs(n, carry):
                got = []
                for u in range(PU):
                    j = n * (2 * PU) + 2 * u
                    r0 = pl.multiple_of(n * (2 * PU * IS), 8)
                    lhs = jnp.concatenate([jnp.concatenate([IM[a, pl.ds(r0 + (2 * u + b) * IS, 64), :].astype(BF) for b in (0, 1)], axis=0) for a in (0, 1)], axis=1)
                    rhs = jnp.concatenate([
                        jnp.concatenate([W[t, j], zero], axis=1),
                        jnp.concatenate([zero, W[t, j + 1]], axis=1)], axis=0)
                    cc = lax.dot_general(lhs, rhs, (((0,), (0,)), ((), ())), preferred_element_type=F32)
                    r = jnp.sum(jnp.abs(cc), axis=0, keepdims=True)
                    got += [r[:, :128], r[:, 128:]]
                for b in range(PU // 4):
                    part[slot, pl.ds(pl.multiple_of(jb * 128 + n * (2 * PU) + 8 * b, 8), 8), :] = jnp.concatenate(got[8 * b:8 * b + 8], axis=0)
                return carry
            lax.fori_loop(0, 128 // (2 * PU), pairs, 0)
        contrib(jb, 1)

        @pl.when(jb <= p)
        def _():
            contrib(big + 1 + jb, 0)
        for w in range(4):
            n = jb * 4 + w

            @pl.when(n != me)
            def _():
                block_to(n).start()
        return carry
    lax.fori_loop(0, big + 1, jstep, 0)

    tl = jnp.concatenate([jnp.sum(part[a].reshape(128, 8, 128), axis=0) for a in (0, 1)], axis=0)
    TL[...] = tl
    TB[me] = tl

    def tell(d, carry):
        total_to(d).start()
        return carry
    lax.fori_loop(1, 32, tell, 0)
    RB[me] = part[:, pl.ds(pl.multiple_of(me * 32, 32), 32), :]

    def heard(d, carry):
        total_to(d).wait()
        return carry
    lax.fori_loop(1, 32, heard, 0)
    for cp in remote:
        cp.wait_send()

    @pl.when(jnp.logical_not(stays))
    def _():
        move.wait_send()

    def sent(n, carry):
        @pl.when(n != me)
        def _():
            block_to(n).wait_send()
        return carry
    lax.fori_loop(0, (big + 1) * 4, sent, 0)

    tb = jnp.sum(TB[...], axis=0)

    def scale(a, ib):
        total = jnp.sum(tb[8 * a:8 * a + 8], axis=0, keepdims=True)
        pos = (ib * 128 + 1 + lax.broadcasted_iota(jnp.int32, (1, 128), 1)).astype(F32)
        return pos / total

    def emit(first, second):
        NB[0] = first
        NB[1] = second

    @pl.when(s <= big)
    def _():
        def take(n, carry):
            @pl.when(n != me)
            def _():
                block_from(n).wait_recv()
            return carry
        lax.fori_loop(0, 32, take, 0)
        norms = jnp.sum(RB[...], axis=0)
        emit(norms[0] * scale(0, p), norms[1] * scale(1, big))

    @pl.when(s > big)
    def _():
        emit(jnp.zeros((32, 128), F32), jnp.zeros((32, 128), F32))

    def home(a):
        ib = (p, big)[a]
        return ib // 2, ib % 2, pltpu.make_async_remote_copy(NB.at[a], out.at[ib % 2], wsend.at[a], wrecv.at[ib % 2], device_id={**at, "row": ib // 2}, device_id_type=MESH)

    for a in (0, 1):
        owner, half, cp = home(a)

        @pl.when(owner == y)
        def _():
            out[half] = NB[a]

        @pl.when(owner != y)
        def _():
            cp.start()
    for h in (0, 1):
        ib = y * 2 + h
        came = (jnp.where(ib < 4, ib, 7 - ib) + 4 - x) % 4

        @pl.when(came != y)
        def _():
            pltpu.make_async_remote_copy(NB.at[h], out.at[h], wsend.at[h], wrecv.at[h], device_id={**at, "row": came}, device_id_type=MESH).wait_recv()
    for a in (0, 1):
        owner, half, cp = home(a)

        @pl.when(owner != y)
        def _():
            cp.wait_send()


def body(query_rows, key_rows, value_rows, out_proj):
    hbm = pl.BlockSpec(memory_space=pl.ANY)
    D = pltpu.SemaphoreType.DMA
    out = pl.pallas_call(
        layer_kernel, out_shape=jax.ShapeDtypeStruct((2, 32, 128), F32), in_specs=[hbm] * 4,
        out_specs=pl.BlockSpec(memory_space=pltpu.VMEM),
        scratch_shapes=[
            pltpu.VMEM((4, 2, 128, 2048), BF), pltpu.VMEM((4, 4, 2, 128, 256), BF), pltpu.VMEM((4, 4, 2, 128, 256), BF), pltpu.VMEM((2, 4, 2048, 128), BF),
            *SCR, pltpu.VMEM((2, 1024, 128), F32), pltpu.VMEM((32, 2, 32, 128), F32), pltpu.VMEM((32, 16, 128), F32),
            pltpu.VMEM((16, 128), F32), pltpu.VMEM((2, 32, 128), F32),
            D((80,)), D((80,)), D((8,)), D((32,)), D((32,)), D((32,)), D((32,)), D((2,)), D((2,))],
        compiler_params=pltpu.CompilerParams(collective_id=0, has_side_effects=True, vmem_limit_bytes=62 * 2**20),
    )(query_rows, key_rows, value_rows, out_proj)
    return out.transpose(0, 2, 1).reshape(256, 32)


def solution(mesh):
    placed = (PS_("row", "width"), PS_("src", "width"), PS_("src", None), PS_(("row", "src"), "width"))
    return jax.shard_map(
        body, mesh=mesh, in_specs=placed, out_specs=PS_("row", ("src", "width")), check_vma=False
    )
```

time: 119 us -> 108 us (0.908)
  the two profiles are of different devices: /device:TPU:30 before, /device:TPU:25 now
where the time goes in v4:
time: 108 us; the launch traced here: 106 us
  Pallas kernels  104 us (96%)
  local copies, waits for them, and re-layouts  1.38 us (1%)
    pallas_call x1, Pallas kernels, body(): pl.pallas_call(layer_kernel, out_shape=jax.ShapeDtypeStruct((2, 32, 128),...  104 us

profile of v4, /device:TPU:25, one launch (start us, length us, event | category | flops | bytes accessed | tf_op | source)
XLA Modules:
  0.0 105.8 jit_solution(10025598391934591538)
XLA Ops:
  0.0 104.4 %shard_map.46 = f32[2,32,128]{2,1,0:T(8,128)} custom-call(bf16[256,2048]{1,0:T(8,128)(2,1)} %qi.1, bf16[128,256]{1,0:T(8,128)(2,1)} %ki.1, bf16[128,1024]{1,0:T(8,128)(2,1)} %vi.1, bf16[256,2048]{1,0:T(8,128)(2,1)} %oi.1), custom_call_target="tpu_custom_call" | custom-call | tf_op jit(solution)/shard_map/pallas_call | solution.py:370
  104.4 1.4 %copy_bitcast_fusion = f32[256,32]{0,1:T(8,128)} fusion(f32[2,32,128]{2,1,0:T(8,128)} %shard_map.46), kind=kLoop, calls=%fused_computation | loop fusion | bytes 65536 | tf_op jit(solution)/shard_map/reshape | solution.py:380

commit v5 on v4

--- a/solution.py
+++ b/solution.py
@@ -17,6 +17,10 @@
 MESH = pl.DeviceIdType.MESH
 
 
+def mixed(a, b):
+    return (a // 2 + b // 2) % 2 * 2 + (a + b) % 2
+
+
 class Links:
     def __init__(self, send, recv, at=None):
         self.send, self.recv, self.n, self.at = send, recv, 0, at
@@ -29,36 +33,34 @@
 
 
 def layer_kernel(qi, ki, vi, oi, out, Q, K, V, OC, P, W, MS, LS, FS, IM, part, RB, TB, TL, NB,
-                 send, recv, local, rsend, rrecv, tsend, trecv, wsend, wrecv):
+                 send, recv, local, rsend, rrecv, tsend, trecv, wsend, wrecv, ready):
     z, y, s = lax.axis_index("width"), lax.axis_index("row"), lax.axis_index("src")
     x, c = s // 2, s % 2
     me = s * 4 + z
-    p = (x + y) % 4
+    p = mixed(x, y)
     big = 7 - p
     at = {"width": z, "row": y, "src": s}
     zu, zd, zf = (z + 1) % 4, (z + 3) % 4, (z + 2) % 4
     yu, yd = (y + 1) % 4, (y + 3) % 4
-    xu, xd = (x + 1) % 4, (x + 3) % 4
+    xu, xd, xf = (x + 1) % 4, (x + 3) % 4, (x + 2) % 4
     su, sd, sib = xu * 2 + c, xd * 2 + c, x * 2 + 1 - c
 
     barrier = pltpu.get_barrier_semaphore()
 
     def peer(n):
-        return {"width": n % 4, "row": (p + 4 - n // 8) % 4, "src": n // 4}
+        return {"width": n % 4, "row": mixed(p, n // 8), "src": n // 4}
 
     def greet(**where):
         pl.semaphore_signal(barrier, inc=1, device_id={**at, **where}, device_id_type=MESH)
 
-    def greet_peer(d, carry):
-        greet(**peer((me + d) % 32))
-        return carry
     for d in range(1, 8):
         greet(src=(s + d) % 8)
     for d in range(1, 4):
         for b in (0, 1):
             greet(row=(y + d) % 4, src=x * 2 + b)
-    lax.fori_loop(1, 32, greet_peer, 0)
-    pl.semaphore_wait(barrier, 44)
+    for w in (zu, zd, zf):
+        greet(width=w)
+    pl.semaphore_wait(barrier, 16)
 
     links = Links(send, recv, at)
     to = links.to
@@ -68,12 +70,11 @@
 
     rows = y * 2 + c
     pair = jnp.where(rows < 4, rows, 7 - rows)
-    goal, slot_to = (pair + 4 - x) % 4, y // 2
+    goal, slot_to = mixed(pair, x), y // 2
     stays = jnp.logical_and(goal == y, slot_to == c)
     q_half = qi.at[pl.ds(c * 128, 128), :]
-    move = to(q_half, Q.at[z, slot_to], row=goal, src=x * 2 + slot_to)
+    move = [to(q_half.at[pl.ds(h * 64, 64), :], Q.at[z, slot_to, pl.ds(h * 64, 64)], row=goal, src=x * 2 + slot_to) for h in (0, 1)]
     keep = pltpu.make_async_copy(q_half, Q.at[z, c], local.at[0])
-    v_own = vi.at[:, pl.ds(z * 256, 256)]
 
     def o_src(b):
         return oi.at[:, pl.ds(b * 128, 128)]
@@ -81,28 +82,27 @@
     def o_dst(ch):
         return OC.at[ch, y, pl.ds(s * 256, 256), :]
     loc_k = pltpu.make_async_copy(ki, K.at[z, x, c], local.at[1])
-    loc_v = pltpu.make_async_copy(v_own, V.at[z, x, c], local.at[2])
+    loc_v = pltpu.make_async_copy(vi, V.at[x, c], local.at[2])
     loc_o = [pltpu.make_async_copy(o_src(s), o_dst(0), local.at[3]), pltpu.make_async_copy(o_src(8 + y * 2 + c), o_dst(1), local.at[4])]
-    kx = [to(ki, K.at[z, x, c], src=(s + d) % 8) for d in range(1, 8)]
-    vx = [to(v_own, V.at[z, x, c], src=(s + d) % 8) for d in range(1, 8)]
+    kx = [to(ki, K.at[z, x, c], src=(s + d) % 8) for d in (2, 4, 6)]
+    vx = [to(vi, V.at[x, c], src=w) for w in (su, sd, sib)]
     oa = [to(o_src((s + d) % 8), o_dst(0), src=(s + d) % 8) for d in range(1, 8)]
     ob = [to(o_src(8 + ((y + d) % 4) * 2 + (c + b) % 2), o_dst(1), row=(y + d) % 4, src=x * 2 + (c + b) % 2) for d in range(1, 4) for b in (0, 1)]
     ob += [to(o_src(8 + y * 2 + 1 - c), o_dst(1), src=sib)]
     ups, downs, other = dict(width=zu), dict(width=zd), dict(src=sib)
     kz = both(K.at[z, :, c], ups, downs)
-    vz = both(V.at[z, :, c], ups, downs)
-    qz = both(Q.at[z, c], ups, downs)
+    qz = [both(Q.at[z, c, pl.ds(h * 64, 64)], ups, downs) for h in (0, 1)]
     kf = both(K.at[zd, pl.ds(0, 2), c], ups) + both(K.at[zu, pl.ds(2, 2), c], downs)
-    vf = both(V.at[zd, pl.ds(0, 2), c], ups) + both(V.at[zu, pl.ds(2, 2), c], downs)
+    vf = both(V.at[xd, c, pl.ds(0, 64)], dict(src=su)) + both(V.at[xu, c, pl.ds(64, 64)], dict(src=sd))
     qf = both(Q.at[zd, c, pl.ds(0, 64)], ups) + both(Q.at[zu, c, pl.ds(64, 64)], downs)
-    kg = [both(K.at[a, :, c], other)[0] for a in (zd, zu, zf)]
-    vg = [both(V.at[a, :, c], other)[0] for a in (zd, zu, zf)]
+    kg = [both(K.at[a, :, c], other)[0] for a in (z, zd, zu, zf)]
+    vg = [both(V.at[a, c], other)[0] for a in (xd, xu, xf)]
     qs = [both(Q.at[a, c], other)[0] for a in (z, zd, zu, zf)]
     oy = both(OC.at[0, y], dict(row=yu), dict(row=yd))
     oyf = both(OC.at[0, yd, pl.ds(0, 1024)], dict(row=yu)) + both(OC.at[0, yu, pl.ds(1024, 1024)], dict(row=yd))
     ow = both(OC.at[1, :, pl.ds(x * 512, 512)], dict(src=su), dict(src=sd))
     owf = both(OC.at[1, pl.ds(0, 2), pl.ds(xd * 512, 512)], dict(src=su)) + both(OC.at[1, pl.ds(2, 2), pl.ds(xu * 512, 512)], dict(src=sd))
-    remote = kx + vx + oa + ob + kz + vz + qz + kf + vf + qf + kg + vg + qs + oy + oyf + ow + owf
+    remote = kx + vx + oa + ob + kz + qz[0] + qz[1] + kf + vf + qf + kg + vg + qs + oy + oyf + ow + owf
 
     def start(*copies):
         for cp in copies:
@@ -120,20 +120,23 @@
 
     @pl.when(jnp.logical_not(stays))
     def _():
-        move.start()
-    start(*loc_o, loc_v, *oa, *ob)
+        start(*move)
+    start(*loc_o, loc_v, *oa)
     loc_k.wait()
     arrived(*kx)
-    start(*kz)
+    start(*kz, kg[0])
+    start(*ob, *vx)
 
     @pl.when(stays)
     def _():
         keep.wait()
 
-    @pl.when(jnp.logical_not(stays))
-    def _():
-        arrived(move)
-    start(qs[0], *qz, *vx)
+    for h in (0, 1):
+        @pl.when(jnp.logical_not(stays))
+        def _():
+            arrived(move[h])
+        start(*qz[h])
+    start(qs[0])
     for cp in loc_o:
         cp.wait()
     loc_v.wait()
@@ -142,7 +145,15 @@
     start(*oy)
     arrived(*ob)
     start(*ow)
-    arrived(qs[0])
+    for h in (0, 1):
+        arrived(kz[h])
+        start(kf[h], kg[1 + h])
+    for h in (0, 1):
+        arrived(vx[h])
+        start(vf[h], vg[h])
+    arrived(qz[0][0])
+    start(qf[0])
+    arrived(kg[0], qs[0])
 
     jl = lax.broadcasted_iota(jnp.int32, (128, 256), 0)
     il = lax.broadcasted_iota(jnp.int32, (128, 256), 1) % 128
@@ -187,45 +198,40 @@
     def zstep(d, carry):
         @pl.when(d == 1)
         def _():
-            arrived(*vx)
-            start(*vz)
-            for h in (0, 1):
-                arrived(kz[h])
-                start(kf[h], kg[h])
-            for h in (0, 1):
-                arrived(qz[h])
-                start(qf[h], qs[1 + h])
-            arrived(kg[0], qs[1])
-
-        @pl.when(d == 2)
-        def _():
+            arrived(qz[0][1], qz[1][1])
+            start(qf[1], qs[2])
+            arrived(qz[1][0])
+            start(qs[1])
             for h in (0, 1):
                 arrived(oy[h])
                 start(oyf[h])
             for h in (0, 1):
                 arrived(ow[h])
                 start(owf[h])
-            for h in (0, 1):
-                arrived(vz[h])
-                start(vf[h], vg[h])
-            arrived(kg[1], qs[2])
+            arrived(kg[1], qs[1])
+
+        @pl.when(d == 2)
+        def _():
+            arrived(*kf)
+            start(kg[3])
+            arrived(*vf)
+            start(vg[2])
+            arrived(kg[2], qs[2])
 
         @pl.when(d == 3)
         def _():
-            arrived(*kf)
-            start(kg[2])
             arrived(*qf)
             start(qs[3])
-            arrived(kg[2], qs[3])
+            arrived(kg[3], qs[3])
         zc = (z + jnp.where(d == 1, 3, jnp.where(d == 2, 1, jnp.where(d == 3, 2, 0)))) % 4
         scores(zc, 0, p, big + 1)
         scores(zc, 1, big, 0)
         return carry
     lax.fori_loop(0, 4, zstep, 0)
 
-    arrived(*vf)
-    start(vg[2])
-    arrived(*vg, *oyf, *owf)
+    arrived(vx[2], *vg, *oyf, *owf)
+    for w in (zu, zd, zf):
+        pl.semaphore_signal(ready, inc=1, device_id={**at, "width": w}, device_id_type=MESH)
 
     def block_to(n):
         return pltpu.make_async_remote_copy(part.at[:, pl.ds(n * 32, 32), :], RB.at[me], rsend.at[n], rrecv.at[me], device_id=peer(n), device_id_type=MESH)
@@ -241,7 +247,7 @@
     def jstep(t, carry):
         jb = jnp.where(t + turn > big, t + turn - big - 1, t + turn)
         for h in range(64):
-            vv = V[h // 16, jb // 2, jb % 2, :, (h // 8 % 2) * 128:(h // 8 % 2 + 1) * 128]
+            vv = V[jb // 2, jb % 2, :, (h // 8) * 128:(h // 8 + 1) * 128]
             oo = jnp.concatenate([OC[a, h // 16, (h % 16) * 128:(h % 16 + 1) * 128, :] for a in (0, 1)], axis=1)
             im = jnp.dot(vv, oo, preferred_element_type=F32)
             for a in (0, 1):
@@ -272,6 +278,20 @@
         @pl.when(jb <= p)
         def _():
             contrib(big + 1 + jb, 0)
+
+        @pl.when(t == 0)
+        def _():
+            pl.semaphore_wait(ready, 3)
+
+        @pl.when(t == 1)
+        def _():
+            for cp in remote:
+                cp.wait_send()
+
+            @pl.when(jnp.logical_not(stays))
+            def _():
+                for cp in move:
+                    cp.wait_send()
         for w in range(4):
             n = jb * 4 + w
 
@@ -294,31 +314,17 @@
     def heard(d, carry):
         total_to(d).wait()
         return carry
-    lax.fori_loop(1, 32, heard, 0)
-    for cp in remote:
-        cp.wait_send()
-
-    @pl.when(jnp.logical_not(stays))
-    def _():
-        move.wait_send()
 
     def sent(n, carry):
         @pl.when(n != me)
         def _():
             block_to(n).wait_send()
         return carry
-    lax.fori_loop(0, (big + 1) * 4, sent, 0)
-
-    tb = jnp.sum(TB[...], axis=0)
-
-    def scale(a, ib):
+
+    def scale(tb, a, ib):
         total = jnp.sum(tb[8 * a:8 * a + 8], axis=0, keepdims=True)
         pos = (ib * 128 + 1 + lax.broadcasted_iota(jnp.int32, (1, 128), 1)).astype(F32)
         return pos / total
-
-    def emit(first, second):
-        NB[0] = first
-        NB[1] = second
 
     @pl.when(s <= big)
     def _():
@@ -328,12 +334,15 @@
                 block_from(n).wait_recv()
             return carry
         lax.fori_loop(0, 32, take, 0)
-        norms = jnp.sum(RB[...], axis=0)
-        emit(norms[0] * scale(0, p), norms[1] * scale(1, big))
+        NB[...] = jnp.sum(RB[...], axis=0)
 
     @pl.when(s > big)
     def _():
-        emit(jnp.zeros((32, 128), F32), jnp.zeros((32, 128), F32))
+        NB[...] = jnp.zeros(NB.shape, F32)
+    lax.fori_loop(1, 32, heard, 0)
+    tb = jnp.sum(TB[...], axis=0)
+    for a, ib in ((0, p), (1, big)):
+        NB[a] = NB[a] * scale(tb, a, ib)
 
     def home(a):
         ib = (p, big)[a]
@@ -349,9 +358,10 @@
         @pl.when(owner != y)
         def _():
             cp.start()
+    lax.fori_loop(0, (big + 1) * 4, sent, 0)
     for h in (0, 1):
         ib = y * 2 + h
-        came = (jnp.where(ib < 4, ib, 7 - ib) + 4 - x) % 4
+        came = mixed(jnp.where(ib < 4, ib, 7 - ib), x)
 
         @pl.when(came != y)
         def _():
@@ -371,10 +381,10 @@
         layer_kernel, out_shape=jax.ShapeDtypeStruct((2, 32, 128), F32), in_specs=[hbm] * 4,
         out_specs=pl.BlockSpec(memory_space=pltpu.VMEM),
         scratch_shapes=[
-            pltpu.VMEM((4, 2, 128, 2048), BF), pltpu.VMEM((4, 4, 2, 128, 256), BF), pltpu.VMEM((4, 4, 2, 128, 256), BF), pltpu.VMEM((2, 4, 2048, 128), BF),
+            pltpu.VMEM((4, 2, 128, 2048), BF), pltpu.VMEM((4, 4, 2, 128, 256), BF), pltpu.VMEM((4, 2, 128, 1024), BF), pltpu.VMEM((2, 4, 2048, 128), BF),
             *SCR, pltpu.VMEM((2, 1024, 128), F32), pltpu.VMEM((32, 2, 32, 128), F32), pltpu.VMEM((32, 16, 128), F32),
             pltpu.VMEM((16, 128), F32), pltpu.VMEM((2, 32, 128), F32),
-            D((80,)), D((80,)), D((8,)), D((32,)), D((32,)), D((32,)), D((32,)), D((2,)), D((2,))],
+            D((80,)), D((80,)), D((8,)), D((32,)), D((32,)), D((32,)), D((32,)), D((2,)), D((2,)), pltpu.SemaphoreType.REGULAR],
         compiler_params=pltpu.CompilerParams(collective_id=0, has_side_effects=True, vmem_limit_bytes=62 * 2**20),
     )(query_rows, key_rows, value_rows, out_proj)
     return out.transpose(0, 2, 1).reshape(256, 32)

time: 108 us -> 103 us (0.954)
  Pallas kernels: 104 us -> 99.9 us
    pallas_call x1, Pallas kernels: 104 us -> 99.9 us  [body(): pl.pallas_call(layer_kernel, out_shape=jax.ShapeDtypeStruct((2, 32, 128),...]
where the time goes in v5:
time: 103 us; the launch traced here: 101 us
  Pallas kernels  99.9 us (97%)
  local copies, waits for them, and re-layouts  1.38 us (1%)
    pallas_call x1, Pallas kernels, body(): pl.pallas_call(layer_kernel, out_shape=jax.ShapeDtypeStruct((2, 32, 128),...  99.9 us

profile of v5, /device:TPU:25, one launch (start us, length us, event | category | flops | bytes accessed | tf_op | source)
XLA Modules:
  0.0 101.2 jit_solution(1805659772732218723)
XLA Ops:
  0.0 99.9 %shard_map.46 = f32[2,32,128]{2,1,0:T(8,128)} custom-call(bf16[256,2048]{1,0:T(8,128)(2,1)} %qi.1, bf16[128,256]{1,0:T(8,128)(2,1)} %ki.1, bf16[128,1024]{1,0:T(8,128)(2,1)} %vi.1, bf16[256,2048]{1,0:T(8,128)(2,1)} %oi.1), custom_call_target="tpu_custom_call" | custom-call | tf_op jit(solution)/shard_map/pallas_call | solution.py:380
  99.9 1.4 %copy_bitcast_fusion = f32[256,32]{0,1:T(8,128)} fusion(f32[2,32,128]{2,1,0:T(8,128)} %shard_map.46), kind=kLoop, calls=%fused_computation | loop fusion | bytes 65536 | tf_op jit(solution)/shard_map/reshape | solution.py:390

commit v6 on v5

--- a/solution.py
+++ b/solution.py
@@ -60,7 +60,6 @@
             greet(row=(y + d) % 4, src=x * 2 + b)
     for w in (zu, zd, zf):
         greet(width=w)
-    pl.semaphore_wait(barrier, 16)
 
     links = Links(send, recv, at)
     to = links.to
@@ -112,7 +111,10 @@
         for cp in copies:
             cp.wait_recv()
 
-    start(loc_k, *kx)
+    start(loc_k, *loc_o, loc_v)
+    part[...] = jnp.zeros(part.shape, F32)
+    pl.semaphore_wait(barrier, 16)
+    start(*kx)
 
     @pl.when(stays)
     def _():
@@ -121,7 +123,7 @@
     @pl.when(jnp.logical_not(stays))
     def _():
         start(*move)
-    start(*loc_o, loc_v, *oa)
+    start(*oa)
     loc_k.wait()
     arrived(*kx)
     start(*kz, kg[0])
@@ -140,7 +142,6 @@
     for cp in loc_o:
         cp.wait()
     loc_v.wait()
-    part[...] = jnp.zeros(part.shape, F32)
     arrived(*oa)
     start(*oy)
     arrived(*ob)
@@ -234,13 +235,14 @@
         pl.semaphore_signal(ready, inc=1, device_id={**at, "width": w}, device_id_type=MESH)
 
     def block_to(n):
-        return pltpu.make_async_remote_copy(part.at[:, pl.ds(n * 32, 32), :], RB.at[me], rsend.at[n], rrecv.at[me], device_id=peer(n), device_id_type=MESH)
-
-    def block_from(n):
-        return pltpu.make_async_remote_copy(part.at[:, pl.ds(n * 32, 32), :], RB.at[n], rsend.at[n], rrecv.at[n], device_id=peer(n), device_id_type=MESH)
-
-    def total_to(d):
-        return pltpu.make_async_remote_copy(TL, TB.at[me], tsend.at[d], trecv.at[d], device_id=peer((me + d) % 32), device_id_type=MESH)
+        return pltpu.make_async_remote_copy(part.at[:, pl.ds(n * 32, 32), :], RB.at[me], rsend.at[n], rrecv, device_id=peer(n), device_id_type=MESH)
+
+    def first_to(d):
+        return pltpu.make_async_remote_copy(TL.at[0], TB.at[z], tsend.at[d], trecv.at[d], device_id={**at, "width": (z + d) % 4}, device_id_type=MESH)
+
+    def second_to(d):
+        n = (s + d) % 8
+        return pltpu.make_async_remote_copy(TL.at[1], TB.at[4 + s], tsend.at[4 + d], trecv.at[4 + d], device_id={"width": z, "row": mixed(p, n // 2), "src": n}, device_id_type=MESH)
 
     turn = (x * (big + 1)) // 4
 
@@ -302,18 +304,20 @@
     lax.fori_loop(0, big + 1, jstep, 0)
 
     tl = jnp.concatenate([jnp.sum(part[a].reshape(128, 8, 128), axis=0) for a in (0, 1)], axis=0)
-    TL[...] = tl
-    TB[me] = tl
-
-    def tell(d, carry):
-        total_to(d).start()
-        return carry
-    lax.fori_loop(1, 32, tell, 0)
-    RB[me] = part[:, pl.ds(pl.multiple_of(me * 32, 32), 32), :]
-
-    def heard(d, carry):
-        total_to(d).wait()
-        return carry
+    TL[0] = tl
+    firsts = [first_to(d) for d in range(1, 4)]
+    seconds = [second_to(d) for d in range(1, 8)]
+    start(*firsts)
+    TB[z] = tl
+
+    @pl.when(s <= big)
+    def _():
+        RB[me] = part[:, pl.ds(pl.multiple_of(me * 32, 32), 32), :]
+    arrived(*firsts)
+    tl = jnp.sum(TB[0:4], axis=0)
+    TL[1] = tl
+    start(*seconds)
+    TB[4 + s] = tl
 
     def sent(n, carry):
         @pl.when(n != me)
@@ -328,19 +332,14 @@
 
     @pl.when(s <= big)
     def _():
-        def take(n, carry):
-            @pl.when(n != me)
-            def _():
-                block_from(n).wait_recv()
-            return carry
-        lax.fori_loop(0, 32, take, 0)
+        pltpu.make_async_remote_copy(RB.at[pl.ds(0, 31)], RB.at[pl.ds(0, 31)], rsend.at[0], rrecv, device_id=at, device_id_type=MESH).wait_recv()
         NB[...] = jnp.sum(RB[...], axis=0)
 
     @pl.when(s > big)
     def _():
         NB[...] = jnp.zeros(NB.shape, F32)
-    lax.fori_loop(1, 32, heard, 0)
-    tb = jnp.sum(TB[...], axis=0)
+    arrived(*seconds)
+    tb = jnp.sum(TB[4:12], axis=0)
     for a, ib in ((0, p), (1, big)):
         NB[a] = NB[a] * scale(tb, a, ib)
 
@@ -359,6 +358,8 @@
         def _():
             cp.start()
     lax.fori_loop(0, (big + 1) * 4, sent, 0)
+    for cp in firsts + seconds:
+        cp.wait_send()
     for h in (0, 1):
         ib = y * 2 + h
         came = mixed(jnp.where(ib < 4, ib, 7 - ib), x)
@@ -382,9 +383,9 @@
         out_specs=pl.BlockSpec(memory_space=pltpu.VMEM),
         scratch_shapes=[
             pltpu.VMEM((4, 2, 128, 2048), BF), pltpu.VMEM((4, 4, 2, 128, 256), BF), pltpu.VMEM((4, 2, 128, 1024), BF), pltpu.VMEM((2, 4, 2048, 128), BF),
-            *SCR, pltpu.VMEM((2, 1024, 128), F32), pltpu.VMEM((32, 2, 32, 128), F32), pltpu.VMEM((32, 16, 128), F32),
-            pltpu.VMEM((16, 128), F32), pltpu.VMEM((2, 32, 128), F32),
-            D((80,)), D((80,)), D((8,)), D((32,)), D((32,)), D((32,)), D((32,)), D((2,)), D((2,)), pltpu.SemaphoreType.REGULAR],
+            *SCR, pltpu.VMEM((2, 1024, 128), F32), pltpu.VMEM((32, 2, 32, 128), F32), pltpu.VMEM((12, 16, 128), F32),
+            pltpu.VMEM((2, 16, 128), F32), pltpu.VMEM((2, 32, 128), F32),
+            D((80,)), D((80,)), D((8,)), D((32,)), D, D((12,)), D((12,)), D((2,)), D((2,)), pltpu.SemaphoreType.REGULAR],
         compiler_params=pltpu.CompilerParams(collective_id=0, has_side_effects=True, vmem_limit_bytes=62 * 2**20),
     )(query_rows, key_rows, value_rows, out_proj)
     return out.transpose(0, 2, 1).reshape(256, 32)

time: 103 us -> 99 us (0.961)
  Pallas kernels: 99.9 us -> 96.8 us
    pallas_call x1, Pallas kernels: 99.9 us -> 96.8 us  [body(): pl.pallas_call(layer_kernel, out_shape=jax.ShapeDtypeStruct((2, 32, 128),...]
where the time goes in v6:
time: 99 us; the launch traced here: 98.2 us
  Pallas kernels  96.8 us (98%)
  local copies, waits for them, and re-layouts  1.38 us (1%)
    pallas_call x1, Pallas kernels, body(): pl.pallas_call(layer_kernel, out_shape=jax.ShapeDtypeStruct((2, 32, 128),...  96.8 us

profile of v6, /device:TPU:25, one launch (start us, length us, event | category | flops | bytes accessed | tf_op | source)
XLA Modules:
  0.0 98.2 jit_solution(3124247202245829737)
XLA Ops:
  0.0 96.8 %shard_map.46 = f32[2,32,128]{2,1,0:T(8,128)} custom-call(bf16[256,2048]{1,0:T(8,128)(2,1)} %qi.1, bf16[128,256]{1,0:T(8,128)(2,1)} %ki.1, bf16[128,1024]{1,0:T(8,128)(2,1)} %vi.1, bf16[256,2048]{1,0:T(8,128)(2,1)} %oi.1), custom_call_target="tpu_custom_call" | custom-call | tf_op jit(solution)/shard_map/pallas_call | solution.py:381
  96.8 1.4 %copy_bitcast_fusion = f32[256,32]{0,1:T(8,128)} fusion(f32[2,32,128]{2,1,0:T(8,128)} %shard_map.46), kind=kLoop, calls=%fused_computation | loop fusion | bytes 65536 | tf_op jit(solution)/shard_map/reshape | solution.py:391

commit v7 on v6

--- a/solution.py
+++ b/solution.py
@@ -196,6 +196,20 @@
             return carry
         lax.fori_loop(0, ib + 1, conv, 0)
 
+    turn = (x * (big + 1)) // 4
+
+    def source(t):
+        return jnp.where(t + turn > big, t + turn - big - 1, t + turn)
+
+    def images(t):
+        jb = source(t)
+        for h in range(64):
+            vv = V[jb // 2, jb % 2, :, (h // 8) * 128:(h // 8 + 1) * 128]
+            oo = jnp.concatenate([OC[a, h // 16, (h % 16) * 128:(h % 16 + 1) * 128, :] for a in (0, 1)], axis=1)
+            im = jnp.dot(vv, oo, preferred_element_type=F32)
+            for a in (0, 1):
+                IM[a, pl.ds(h, 128, stride=IS), :] = im[:, a * 128:(a + 1) * 128]
+
     def zstep(d, carry):
         @pl.when(d == 1)
         def _():
@@ -223,14 +237,15 @@
         def _():
             arrived(*qf)
             start(qs[3])
-            arrived(kg[3], qs[3])
+            arrived(kg[3], vx[2], *vg, *oyf, *owf)
+            images(0)
+            arrived(qs[3])
         zc = (z + jnp.where(d == 1, 3, jnp.where(d == 2, 1, jnp.where(d == 3, 2, 0)))) % 4
         scores(zc, 0, p, big + 1)
         scores(zc, 1, big, 0)
         return carry
     lax.fori_loop(0, 4, zstep, 0)
 
-    arrived(vx[2], *vg, *oyf, *owf)
     for w in (zu, zd, zf):
         pl.semaphore_signal(ready, inc=1, device_id={**at, "width": w}, device_id_type=MESH)
 
@@ -244,16 +259,9 @@
         n = (s + d) % 8
         return pltpu.make_async_remote_copy(TL.at[1], TB.at[4 + s], tsend.at[4 + d], trecv.at[4 + d], device_id={"width": z, "row": mixed(p, n // 2), "src": n}, device_id_type=MESH)
 
-    turn = (x * (big + 1)) // 4
 
     def jstep(t, carry):
-        jb = jnp.where(t + turn > big, t + turn - big - 1, t + turn)
-        for h in range(64):
-            vv = V[jb // 2, jb % 2, :, (h // 8) * 128:(h // 8 + 1) * 128]
-            oo = jnp.concatenate([OC[a, h // 16, (h % 16) * 128:(h % 16 + 1) * 128, :] for a in (0, 1)], axis=1)
-            im = jnp.dot(vv, oo, preferred_element_type=F32)
-            for a in (0, 1):
-                IM[a, pl.ds(h, 128, stride=IS), :] = im[:, a * 128:(a + 1) * 128]
+        jb = source(t)
 
         def contrib(t, slot):
             zero = jnp.zeros((64, 128), BF)
@@ -300,6 +308,10 @@
             @pl.when(n != me)
             def _():
                 block_to(n).start()
+
+        @pl.when(t < big)
+        def _():
+            images(t + 1)
         return carry
     lax.fori_loop(0, big + 1, jstep, 0)
 

time: 99 us -> 98 us (0.990)
  Pallas kernels: 96.8 us -> 95.8 us
    pallas_call x1, Pallas kernels: 96.8 us -> 95.8 us  [body(): pl.pallas_call(layer_kernel, out_shape=jax.ShapeDtypeStruct((2, 32, 128),...]
where the time goes in v7:
time: 98 us; the launch traced here: 97.2 us
  Pallas kernels  95.8 us (98%)
  local copies, waits for them, and re-layouts  1.38 us (1%)
    pallas_call x1, Pallas kernels, body(): pl.pallas_call(layer_kernel, out_shape=jax.ShapeDtypeStruct((2, 32, 128),...  95.8 us

profile of v7, /device:TPU:25, one launch (start us, length us, event | category | flops | bytes accessed | tf_op | source)
XLA Modules:
  0.0 97.2 jit_solution(4275009864691935934)
XLA Ops:
  0.0 95.8 %shard_map.46 = f32[2,32,128]{2,1,0:T(8,128)} custom-call(bf16[256,2048]{1,0:T(8,128)(2,1)} %qi.1, bf16[128,256]{1,0:T(8,128)(2,1)} %ki.1, bf16[128,1024]{1,0:T(8,128)(2,1)} %vi.1, bf16[256,2048]{1,0:T(8,128)(2,1)} %oi.1), custom_call_target="tpu_custom_call" | custom-call | tf_op jit(solution)/shard_map/pallas_call | solution.py:393
  95.8 1.4 %copy_bitcast_fusion = f32[256,32]{0,1:T(8,128)} fusion(f32[2,32,128]{2,1,0:T(8,128)} %shard_map.46), kind=kLoop, calls=%fused_computation | loop fusion | bytes 65536 | tf_op jit(solution)/shard_map/reshape | solution.py:403

commit v8 on v7

--- a/solution.py
+++ b/solution.py
@@ -9,9 +9,9 @@
 NEG = -1e30
 PS, IS = 17, 65
 
-SCR = [pltpu.VMEM((8, 128 * PS, 128), F32), pltpu.VMEM((9, 128, 64, 128), BF),
+SCR = [pltpu.VMEM((8, 128 * PS + 16, 128), F32), pltpu.VMEM((9, 128, 64, 128), BF),
        pltpu.VMEM((8, 16, 128), F32), pltpu.VMEM((8, 16, 128), F32), pltpu.VMEM((8, 16, 128), F32),
-       pltpu.VMEM((2, 128 * IS, 128), F32)]
+       pltpu.VMEM((2, 128 * IS + 64, 128), F32)]
 
 
 MESH = pl.DeviceIdType.MESH

time: 98 us -> 98 us (level)
  no operation moved by 1% of the time
where the time goes in v8:
time: 98 us; the launch traced here: 97.2 us
  Pallas kernels  95.8 us (98%)
  local copies, waits for them, and re-layouts  1.38 us (1%)
    pallas_call x1, Pallas kernels, body(): pl.pallas_call(layer_kernel, out_shape=jax.ShapeDtypeStruct((2, 32, 128),...  95.8 us

profile of v8, /device:TPU:25, one launch (start us, length us, event | category | flops | bytes accessed | tf_op | source)
XLA Modules:
  0.0 97.2 jit_solution(7339125882020597337)
XLA Ops:
  0.0 95.8 %shard_map.46 = f32[2,32,128]{2,1,0:T(8,128)} custom-call(bf16[256,2048]{1,0:T(8,128)(2,1)} %qi.1, bf16[128,256]{1,0:T(8,128)(2,1)} %ki.1, bf16[128,1024]{1,0:T(8,128)(2,1)} %vi.1, bf16[256,2048]{1,0:T(8,128)(2,1)} %oi.1), custom_call_target="tpu_custom_call" | custom-call | tf_op jit(solution)/shard_map/pallas_call | solution.py:393
  95.8 1.4 %copy_bitcast_fusion = f32[256,32]{0,1:T(8,128)} fusion(f32[2,32,128]{2,1,0:T(8,128)} %shard_map.46), kind=kLoop, calls=%fused_computation | loop fusion | bytes 65536 | tf_op jit(solution)/shard_map/reshape | solution.py:403
